TPU v7x, 256 devices: a whole 4x4x8 slice. The times are simulated.
256 devices in a mesh: seq: 32 (over x, y, core), mp: 8 (over z).
Axes of the slice: x: 4, y: 4, z: 8, core: 2. Of those that a mesh axis runs over, the one named last changes fastest.
Arguments:
- x_branch: bfloat16 [8192, 8192], P('seq', 'mp'), may hold values from -6 to 6
- z_branch: bfloat16 [8192, 8192], P('seq', 'mp'), may hold values from -6 to 6
- conv_weight: float32 [4, 8192], P(None, 'mp'), may hold values from -3 to 3
- conv_bias: float32 [8192], P('mp'), may hold values from -0.5 to 0.5
- xproj_weight: bfloat16 [8192, 544], P('mp'), may hold values from -0.0625 to 0.0625
- dt_weight: bfloat16 [512, 8192], P(None, 'mp'), may hold values from -0.25 to 0.25
- dt_bias: float32 [8192], P('mp'), may hold values from -4 to -2
- decay_rate: float32 [16, 8192], P(None, 'mp'), may hold values from 0.00024414062 to 2
- skip_gain: float32 [8192], P('mp'), may hold values from 0.5 to 1.5
- query_rows: bfloat16 [8192, 8192], P('seq', 'mp'), may hold values from -6 to 6
- key_rows: bfloat16 [8192, 1024], P('seq', 'mp'), may hold values from -6 to 6
- value_rows: bfloat16 [8192, 1024], P('seq', 'mp'), may hold values from -6 to 6
- lengths: int32 [4], replicated, may hold values from 1 to 4096, as said below
- destination: int32 [8192], replicated, may hold values from 0 to 8191, as said below
Outputs:
- mamba_out: bfloat16 [8192, 8192], P('seq', 'mp')
- regrouped: bfloat16 [8192, 8192], P('seq', 'mp')
Inputs may be any that keep to these rules, and one draw needn't show every extreme that they name: The 4 lengths sum to 8192, and the second of them equals 4096. destination is a permutation of 0 to 8191. Cut each aligned block of 256 positions into 32 runs of 8 consecutive positions: each run goes in order to consecutive rows of one aligned target block, the runs of block i to the rows that start at i * 8 within their target blocks, and the 32 runs of one block go to 32 different target blocks.
All inputs are finite; a program needn't handle non-finite values.
Results may differ from a plain program's by a relative error of at most 0.02.
Values may be sent and summed in bfloat16 or wider, within the bound.
A program may use at most 128 MiB of HBM per device.

v0:
```python
import jax
import jax.numpy as jnp
from jax import lax
from jax.sharding import Mesh
from jax.sharding import PartitionSpec as P

HD = 128
SEQ = ("seq_0", "seq_1", "seq_2")


masked_score = -1e30


def shifted_2(value, axis, steps):
    count = lax.axis_size(axis)
    first, last = (max(0, -steps), min(count, count - steps))
    return lax.ppermute(value, axis, [(source, source + steps) for source in range(first, last)])


def sent_to_all(value, axis):
    copies = jnp.broadcast_to(value, (lax.axis_size(axis), *value.shape))
    return lax.all_to_all(copies, axis, split_axis=0, concat_axis=0, tiled=True)


def of_everyone(value, axis):
    return sent_to_all(value, axis).astype(jnp.float32).sum(axis=0)


def nothing_yet(value, identity):
    return jax.tree.map(
        lambda a, e: jnp.broadcast_to(jnp.asarray(e, a.dtype), a.shape), value, identity
    )


def entering(value, axes, combine, identity):
    before = start = nothing_yet(value, identity)
    total = value
    for axis in reversed(axes):
        length, place = (lax.axis_size(axis), lax.axis_index(axis))
        pieces = jax.tree.map(
            lambda part, kind: lax.all_gather(part.astype(kind), axis),
            total,
            jax.tree.map(lambda a: jnp.bfloat16 if a.dtype == jnp.float32 else a.dtype, value),
        )
        inside, total = (start, start)
        for k in range(length):
            passed = k < place
            total = combine(
                total, jax.tree.map(lambda part, own: part[k].astype(own.dtype), pieces, value)
            )
            inside = jax.tree.map(lambda new, old: jnp.where(passed, new, old), total, inside)
        before = combine(inside, before)
    return before


def doc_lookup(lengths, places):
    doc_ends = jnp.cumsum(lengths)
    starts = doc_ends - lengths
    doc_ids = jnp.sum((places[:, None] >= doc_ends[None, :]).astype(jnp.int32), axis=1)
    at_start = jnp.any(places[:, None] == starts[None, :], axis=1)
    return (doc_ids, at_start)


def chain_states(earlier, latter):
    return (earlier[0] * latter[0], latter[0] * earlier[1] + latter[1])


def block_decay(step_col, keep_col, decay_rate):
    return jnp.exp(-step_col[:, None, :] * decay_rate[None, :, :]) * keep_col[:, None, None]


def mamba_mixer(
    x_branch,
    z_branch,
    conv_weight,
    conv_bias,
    xproj_weight,
    dt_weight,
    dt_bias,
    decay_rate,
    skip_gain,
    lengths,
):
    tok_count = x_branch.shape[0]
    channels = x_branch.shape[1]
    tap_count = conv_weight.shape[0]
    low_rank = dt_weight.shape[0]
    states = decay_rate.shape[0]
    position = lax.axis_index(SEQ)
    anchor = position * tok_count
    places = anchor + jnp.arange(tok_count, dtype=jnp.int32)
    doc_ids, at_start = doc_lookup(lengths, places)
    earlier_rows = shifted_2(x_branch[tok_count - (tap_count - 1) :], SEQ, 1)
    extended = jnp.concatenate([earlier_rows, x_branch], axis=0).astype(jnp.float32)
    ext_docs, unused = doc_lookup(
        lengths, anchor - (tap_count - 1) + jnp.arange(tok_count + tap_count - 1, dtype=jnp.int32)
    )
    conv_sum = conv_bias[None, :] + jnp.zeros((tok_count, channels), jnp.float32)
    for lag_step in range(tap_count):
        begin = tap_count - 1 - lag_step
        window = extended[begin : begin + tok_count]
        same_doc = ext_docs[begin : begin + tok_count] == doc_ids
        conv_sum = conv_sum + conv_weight[lag_step][None, :] * jnp.where(
            same_doc[:, None], window, 0.0
        )
    inner_act = jax.nn.silu(conv_sum).astype(jnp.bfloat16)
    partial_value = jnp.dot(inner_act, xproj_weight, preferred_element_type=jnp.float32)
    projected = of_everyone(partial_value.astype(jnp.bfloat16), "mp").astype(jnp.float32)
    dt_low = projected[:, :low_rank].astype(jnp.bfloat16)
    step_size = jax.nn.softplus(
        jnp.dot(dt_low, dt_weight, preferred_element_type=jnp.float32) + dt_bias[None, :]
    )
    inner_float = inner_act.astype(jnp.float32)
    run_length = 16
    block_count = tok_count // run_length
    step_blocks = step_size.reshape(block_count, run_length, channels)
    drive_term = (step_size * inner_float).reshape(block_count, run_length, channels)
    b_blocks = projected[:, low_rank : low_rank + states].reshape(block_count, run_length, states)
    c_blocks = projected[:, low_rank + states :].reshape(block_count, run_length, states)
    keep_blocks = jnp.where(at_start, 0.0, 1.0).astype(jnp.float32).reshape(block_count, run_length)
    carried = jnp.zeros((block_count, states, channels), jnp.float32)
    decayed = jnp.ones((block_count, states, channels), jnp.float32)
    for offset in range(run_length):
        decay_now = block_decay(step_blocks[:, offset], keep_blocks[:, offset], decay_rate)
        carried = (
            decay_now * carried + drive_term[:, offset, None, :] * b_blocks[:, offset, :, None]
        )
        decayed = decay_now * decayed
    inclusive = lax.associative_scan(chain_states, (decayed, carried), axis=0)
    device_state = (inclusive[0][-1], inclusive[1][-1])
    identity = (
        jnp.ones((states, channels), jnp.float32),
        jnp.zeros((states, channels), jnp.float32),
    )
    inbound = entering(device_state, SEQ, chain_states, identity)
    incoming = inbound[1]
    start_decay = jnp.concatenate(
        [jnp.ones((1, states, channels), jnp.float32), inclusive[0][:-1]], axis=0
    )
    start_state = jnp.concatenate(
        [jnp.zeros((1, states, channels), jnp.float32), inclusive[1][:-1]], axis=0
    )
    carried = start_decay * incoming[None] + start_state
    outputs = []
    for offset in range(run_length):
        decay_now = block_decay(step_blocks[:, offset], keep_blocks[:, offset], decay_rate)
        carried = (
            decay_now * carried + drive_term[:, offset, None, :] * b_blocks[:, offset, :, None]
        )
        outputs.append(jnp.sum(c_blocks[:, offset, :, None] * carried, axis=1))
    scanned = (
        jnp.stack(outputs, axis=1).reshape(tok_count, channels) + skip_gain[None, :] * inner_float
    )
    mamba_out = (scanned * jax.nn.silu(z_branch.astype(jnp.float32))).astype(jnp.bfloat16)
    return (mamba_out, doc_ids)


def absorb(
    carried, query_heads, query_places, query_docs, key_block, value_block, key_start, lengths
):
    key_count = key_block.shape[0]
    kv_local = query_heads.shape[1]
    head_size = query_heads.shape[3]
    key_places = key_start + jnp.arange(key_count, dtype=jnp.int32)
    key_docs, unused = doc_lookup(lengths, key_places)
    factor = head_size ** (-0.5)
    scores = (
        jnp.einsum(
            "qhgd,khd->hgqk",
            query_heads,
            key_block.reshape(key_count, kv_local, head_size),
            preferred_element_type=jnp.float32,
        )
        * factor
    )
    visible = (
        (key_places[None, :] <= query_places[:, None])
        & (key_docs[None, :] == query_docs[:, None])
        & (key_places[None, :] >= 0)
    )
    scores = jnp.where(visible[None, None], scores, masked_score)
    best_score, weight_sum, summed = carried
    new_best = jnp.maximum(best_score, jnp.max(scores, axis=3))
    weights = jnp.where(visible[None, None], jnp.exp(scores - new_best[..., None]), 0.0)
    rescale = jnp.exp(best_score - new_best)
    weight_sum = weight_sum * rescale + jnp.sum(weights, axis=3)
    product = jnp.einsum(
        "hgqk,khd->qhgd",
        weights.astype(jnp.bfloat16),
        value_block.reshape(key_count, kv_local, head_size),
        preferred_element_type=jnp.float32,
    )
    summed = summed * jnp.transpose(rescale, (2, 0, 1))[..., None] + product
    return (new_best, weight_sum, summed)


def send_runs(rows, destination, tok_count, n_seq, anchor):
    run_rows = tok_count // n_seq
    own_targets = (
        lax.dynamic_slice_in_dim(destination, anchor, tok_count, 0).reshape(n_seq, run_rows)[:, 0]
        // tok_count
    )
    send_order = jnp.argsort(own_targets, stable=True)
    return rows.reshape(n_seq, run_rows, rows.shape[1])[send_order].reshape(
        tok_count, rows.shape[1]
    )


def attention_mixer(query_rows, key_rows, value_rows, doc_ids, lengths, destination):
    tok_count = query_rows.shape[0]
    n_seq = lax.axis_size(SEQ)
    reach_count = n_seq // 2
    kv_local = key_rows.shape[1] // HD
    group_size = query_rows.shape[1] // key_rows.shape[1]
    position = lax.axis_index(SEQ)
    anchor = position * tok_count
    initial = (
        jnp.full((kv_local, group_size, tok_count), masked_score, jnp.float32),
        jnp.zeros((kv_local, group_size, tok_count), jnp.float32),
        jnp.zeros((tok_count, kv_local, group_size, HD), jnp.float32),
    )
    places = anchor + jnp.arange(tok_count, dtype=jnp.int32)
    query_heads = query_rows.reshape(tok_count, kv_local, group_size, HD)
    last_place = anchor + tok_count - 1
    first_doc = doc_ids[0]

    def absorb_if_needed(carried, key_block, value_block, key_start):
        key_count = key_block.shape[0]
        tail_place = jnp.reshape(key_start + key_count - 1, (1,))
        tail_doc = doc_lookup(lengths, tail_place)[0][0]
        wanted = (
            (key_start <= last_place) & (tail_doc >= first_doc) & (key_start + key_count - 1 >= 0)
        )
        return lax.cond(
            wanted,
            lambda kept_carry: absorb(
                kept_carry, query_heads, places, doc_ids, key_block, value_block, key_start, lengths
            ),
            lambda kept_carry: kept_carry,
            carried,
        )

    carried = absorb_if_needed(initial, key_rows, value_rows, anchor)

    def look_back(lag_step, loop_carry):
        attn_carry, moving = loop_carry
        shifted = shifted_2((moving[0], moving[1]), SEQ, 1)
        moving = (shifted[0], shifted[1])
        attn_carry = absorb_if_needed(
            attn_carry, moving[0], moving[1], anchor - lag_step * tok_count
        )
        return (attn_carry, moving)

    carried, unused = lax.fori_loop(
        1, reach_count + 1, look_back, (carried, (key_rows, value_rows))
    )
    best_score, weight_sum, summed = carried
    attended = (
        (summed / jnp.transpose(weight_sum, (2, 0, 1))[..., None])
        .reshape(tok_count, kv_local * group_size * HD)
        .astype(jnp.bfloat16)
    )
    outgoing = send_runs(attended, destination, tok_count, n_seq, anchor)
    return lax.all_to_all(outgoing, SEQ, split_axis=0, concat_axis=0, tiled=True)


def local(
    x_branch,
    z_branch,
    conv_weight,
    conv_bias,
    xproj_weight,
    dt_weight,
    dt_bias,
    decay_rate,
    skip_gain,
    query_rows,
    key_rows,
    value_rows,
    lengths,
    destination,
):
    mamba_out, doc_ids = mamba_mixer(
        x_branch,
        z_branch,
        conv_weight,
        conv_bias,
        xproj_weight,
        dt_weight,
        dt_bias,
        decay_rate,
        skip_gain,
        lengths,
    )
    regrouped = attention_mixer(query_rows, key_rows, value_rows, doc_ids, lengths, destination)
    return (mamba_out, regrouped)


def solution(mesh):
    torus = Mesh(mesh.devices.reshape(4, 4, 2, mesh.shape["mp"]), ("seq_0", "seq_1", "seq_2", "mp"))
    in_specs = (
        P(SEQ, "mp"),
        P(SEQ, "mp"),
        P(None, "mp"),
        P("mp"),
        P("mp", None),
        P(None, "mp"),
        P("mp"),
        P(None, "mp"),
        P("mp"),
        P(SEQ, "mp"),
        P(SEQ, "mp"),
        P(SEQ, "mp"),
        P(),
        P(),
    )
    out_specs = (P(SEQ, "mp"), P(SEQ, "mp"))
    return jax.shard_map(local, mesh=torus, in_specs=in_specs, out_specs=out_specs, check_vma=False)
```

profile of v0, /device:TPU:32, one launch (start us, length us, event | category | flops | bytes accessed | tf_op | source)
XLA Modules:
  0.0 524.9 jit_solution(1361201450512699606)
XLA Ops:
  10.1 3.7 conditional.2
  13.9 178.1 %while.27 = (s32[]{:T(128)}, f32[1,8,256]{2,1,0:T(8,128)}, f32[1,8,256]{2,1,0:T(8,128)S(1)}, f32[256,1,8,128]{3,0,2,1:T(8,128)S(1)}, bf16[256,128]{1,0:T(8,128)(...) while((s32[]{:T(128)}, f32[1,8,256]{2,1,0:T(8,128)}, ...), condition=%wide.region_37.38_spmd.clone.clone, body=%wide.region_29.0_spmd.clone.clone.sunk | while | flops 276047648 | bytes 10234911 | solution.py:254
  13.9 3.8 collective-permute-start
  17.6 1.9 collective-permute-start.1
  21.6 8.0 %collective-permute-start = (bf16[256,128]{1,0:T(8,128)(2,1)S(1)}, bf16[256,128]{1,0:T(8,128)(2,1)S(1)}, u32[]{:S(2)}, u32[]{:S(2)}) collective-permute-start(bf16[256,128]{1,0:T(8,128)(2,1)S(1)} %get-tuple-element.1034), channel_id=1, source_target_pairs={{0,8},{8,16},{16,24},{24,32},{32,40},{40,48},{48,56},{56,64},{64,7... | collective-permute-start | bytes 196616 | tf_op jit(solution)/shard_map/while/body/eval_jaxpr/ppermute | solution.py:17
  29.6 3.6 collective-permute-start.1
  35.3 1.9 collective-permute-start
  37.2 8.1 %collective-permute-start.1 = (bf16[256,128]{1,0:T(8,128)(2,1)S(1)}, bf16[256,128]{1,0:T(8,128)(2,1)S(1)}, u32[]{:S(2)}, u32[]{:S(2)}) collective-permute-start(bf16[256,128]{1,0:T(8,128)(2,1)S(1)} %get-tuple-element.1035), channel_id=1, source_target_pairs={{0,8},{8,16},{16,24},{24,32},{32,40},{40,48},{48,56},{56,64},{64,7... | collective-permute-start | bytes 196616 | tf_op jit(solution)/shard_map/while/body/eval_jaxpr/ppermute | solution.py:17
  47.3 1.9 collective-permute-start
  49.2 3.6 collective-permute-start.1
  54.8 6.1 %collective-permute-start = (bf16[256,128]{1,0:T(8,128)(2,1)S(1)}, bf16[256,128]{1,0:T(8,128)(2,1)S(1)}, u32[]{:S(2)}, u32[]{:S(2)}) collective-permute-start(bf16[256,128]{1,0:T(8,128)(2,1)S(1)} %get-tuple-element.1034), channel_id=1, source_target_pairs={{0,8},{8,16},{16,24},{24,32},{32,40},{40,48},{48,56},{56,64},{64,7... | collective-permute-start | bytes 196616 | tf_op jit(solution)/shard_map/while/body/eval_jaxpr/ppermute | solution.py:17
  60.9 5.2 collective-permute-start.1
  68.2 1.9 collective-permute-start
  70.1 8.1 %collective-permute-start.1 = (bf16[256,128]{1,0:T(8,128)(2,1)S(1)}, bf16[256,128]{1,0:T(8,128)(2,1)S(1)}, u32[]{:S(2)}, u32[]{:S(2)}) collective-permute-start(bf16[256,128]{1,0:T(8,128)(2,1)S(1)} %get-tuple-element.1035), channel_id=1, source_target_pairs={{0,8},{8,16},{16,24},{24,32},{32,40},{40,48},{48,56},{56,64},{64,7... | collective-permute-start | bytes 196616 | tf_op jit(solution)/shard_map/while/body/eval_jaxpr/ppermute | solution.py:17
  80.2 1.9 collective-permute-start
  82.1 3.6 collective-permute-start.1
  89.6 9.9 %collective-permute-start.1 = (bf16[256,128]{1,0:T(8,128)(2,1)S(1)}, bf16[256,128]{1,0:T(8,128)(2,1)S(1)}, u32[]{:S(2)}, u32[]{:S(2)}) collective-permute-start(bf16[256,128]{1,0:T(8,128)(2,1)S(1)} %get-tuple-element.1035), channel_id=1, source_target_pairs={{0,8},{8,16},{16,24},{24,32},{32,40},{40,48},{48,56},{56,64},{64,7... | collective-permute-start | bytes 196616 | tf_op jit(solution)/shard_map/while/body/eval_jaxpr/ppermute | solution.py:17
  103.5 5.7 %collective-permute-start.1 = (bf16[256,128]{1,0:T(8,128)(2,1)S(1)}, bf16[256,128]{1,0:T(8,128)(2,1)S(1)}, u32[]{:S(2)}, u32[]{:S(2)}) collective-permute-start(bf16[256,128]{1,0:T(8,128)(2,1)S(1)} %get-tuple-element.1035), channel_id=1, source_target_pairs={{0,8},{8,16},{16,24},{24,32},{32,40},{40,48},{48,56},{56,64},{64,7... | collective-permute-start | bytes 196616 | tf_op jit(solution)/shard_map/while/body/eval_jaxpr/ppermute | solution.py:17
  111.3 1.9 collective-permute-start
  113.2 5.7 %collective-permute-start.1 = (bf16[256,128]{1,0:T(8,128)(2,1)S(1)}, bf16[256,128]{1,0:T(8,128)(2,1)S(1)}, u32[]{:S(2)}, u32[]{:S(2)}) collective-permute-start(bf16[256,128]{1,0:T(8,128)(2,1)S(1)} %get-tuple-element.1035), channel_id=1, source_target_pairs={{0,8},{8,16},{16,24},{24,32},{32,40},{40,48},{48,56},{56,64},{64,7... | collective-permute-start | bytes 196616 | tf_op jit(solution)/shard_map/while/body/eval_jaxpr/ppermute | solution.py:17
  122.9 5.7 %collective-permute-start.1 = (bf16[256,128]{1,0:T(8,128)(2,1)S(1)}, bf16[256,128]{1,0:T(8,128)(2,1)S(1)}, u32[]{:S(2)}, u32[]{:S(2)}) collective-permute-start(bf16[256,128]{1,0:T(8,128)(2,1)S(1)} %get-tuple-element.1035), channel_id=1, source_target_pairs={{0,8},{8,16},{16,24},{24,32},{32,40},{40,48},{48,56},{56,64},{64,7... | collective-permute-start | bytes 196616 | tf_op jit(solution)/shard_map/while/body/eval_jaxpr/ppermute | solution.py:17
  130.6 1.9 collective-permute-start
  132.5 5.7 %collective-permute-start.1 = (bf16[256,128]{1,0:T(8,128)(2,1)S(1)}, bf16[256,128]{1,0:T(8,128)(2,1)S(1)}, u32[]{:S(2)}, u32[]{:S(2)}) collective-permute-start(bf16[256,128]{1,0:T(8,128)(2,1)S(1)} %get-tuple-element.1035), channel_id=1, source_target_pairs={{0,8},{8,16},{16,24},{24,32},{32,40},{40,48},{48,56},{56,64},{64,7... | collective-permute-start | bytes 196616 | tf_op jit(solution)/shard_map/while/body/eval_jaxpr/ppermute | solution.py:17
  140.3 6.0 %collective-permute-start = (bf16[256,128]{1,0:T(8,128)(2,1)S(1)}, bf16[256,128]{1,0:T(8,128)(2,1)S(1)}, u32[]{:S(2)}, u32[]{:S(2)}) collective-permute-start(bf16[256,128]{1,0:T(8,128)(2,1)S(1)} %get-tuple-element.1034), channel_id=1, source_target_pairs={{0,8},{8,16},{16,24},{24,32},{32,40},{40,48},{48,56},{56,64},{64,7... | collective-permute-start | bytes 196616 | tf_op jit(solution)/shard_map/while/body/eval_jaxpr/ppermute | solution.py:17
  146.3 5.7 %collective-permute-start.1 = (bf16[256,128]{1,0:T(8,128)(2,1)S(1)}, bf16[256,128]{1,0:T(8,128)(2,1)S(1)}, u32[]{:S(2)}, u32[]{:S(2)}) collective-permute-start(bf16[256,128]{1,0:T(8,128)(2,1)S(1)} %get-tuple-element.1035), channel_id=1, source_target_pairs={{0,8},{8,16},{16,24},{24,32},{32,40},{40,48},{48,56},{56,64},{64,7... | collective-permute-start | bytes 196616 | tf_op jit(solution)/shard_map/while/body/eval_jaxpr/ppermute | solution.py:17
  154.1 1.9 collective-permute-start
  156.0 10.2 %collective-permute-start.1 = (bf16[256,128]{1,0:T(8,128)(2,1)S(1)}, bf16[256,128]{1,0:T(8,128)(2,1)S(1)}, u32[]{:S(2)}, u32[]{:S(2)}) collective-permute-start(bf16[256,128]{1,0:T(8,128)(2,1)S(1)} %get-tuple-element.1035), channel_id=1, source_target_pairs={{0,8},{8,16},{16,24},{24,32},{32,40},{40,48},{48,56},{56,64},{64,7... | collective-permute-start | bytes 196616 | tf_op jit(solution)/shard_map/while/body/eval_jaxpr/ppermute | solution.py:17
  168.2 1.9 collective-permute-start
  170.1 5.7 %collective-permute-start.1 = (bf16[256,128]{1,0:T(8,128)(2,1)S(1)}, bf16[256,128]{1,0:T(8,128)(2,1)S(1)}, u32[]{:S(2)}, u32[]{:S(2)}) collective-permute-start(bf16[256,128]{1,0:T(8,128)(2,1)S(1)} %get-tuple-element.1035), channel_id=1, source_target_pairs={{0,8},{8,16},{16,24},{24,32},{32,40},{40,48},{48,56},{56,64},{64,7... | collective-permute-start | bytes 196616 | tf_op jit(solution)/shard_map/while/body/eval_jaxpr/ppermute | solution.py:17
  177.8 6.4 %collective-permute-start = (bf16[256,128]{1,0:T(8,128)(2,1)S(1)}, bf16[256,128]{1,0:T(8,128)(2,1)S(1)}, u32[]{:S(2)}, u32[]{:S(2)}) collective-permute-start(bf16[256,128]{1,0:T(8,128)(2,1)S(1)} %get-tuple-element.1034), channel_id=1, source_target_pairs={{0,8},{8,16},{16,24},{24,32},{32,40},{40,48},{48,56},{56,64},{64,7... | collective-permute-start | bytes 196616 | tf_op jit(solution)/shard_map/while/body/eval_jaxpr/ppermute | solution.py:17
  184.2 5.7 %collective-permute-start.1 = (bf16[256,128]{1,0:T(8,128)(2,1)S(1)}, bf16[256,128]{1,0:T(8,128)(2,1)S(1)}, u32[]{:S(2)}, u32[]{:S(2)}) collective-permute-start(bf16[256,128]{1,0:T(8,128)(2,1)S(1)} %get-tuple-element.1035), channel_id=1, source_target_pairs={{0,8},{8,16},{16,24},{24,32},{32,40},{40,48},{48,56},{56,64},{64,7... | collective-permute-start | bytes 196616 | tf_op jit(solution)/shard_map/while/body/eval_jaxpr/ppermute | solution.py:17
  196.9 40.3 %all-to-all-start.1 = ((bf16[32,8,1024]{2,1,0:T(8,128)(2,1)}), bf16[32,8,1024]{2,1,0:T(8,128)(2,1)S(1)}, u32[]{:S(2)}, u32[]{:S(2)}) async-start(bf16[32,8,1024]{2,1,0:T(8,128)(2,1)} %gather_fusion), calls=%async_computation.1 | async-start | bytes 1048576 | tf_op jit(solution)/shard_map/all_to_all | solution.py:264
  239.5 8.7 %all-to-all-done.1 = bf16[32,8,1024]{2,1,0:T(8,128)(2,1)S(1)} async-done(((bf16[32,8,1024]{2,1,0:T(8,128)(2,1)}), bf16[32,8,1024]{2,1,0:T(8,128)(2,1)S(1)}, u32[]{:S(2)}, u32[]{:S(2)}) %all-to-all-start.1) | async-done | bytes 524320 | tf_op jit(solution)/shard_map/all_to_all | solution.py:264
  249.8 8.6 %all-to-all-start = ((bf16[8,256,544]{1,2,0:T(8,128)(2,1)}), bf16[8,256,544]{1,2,0:T(8,128)(2,1)}, u32[]{:S(2)}, u32[]{:S(2)}) async-start(bf16[8,256,544]{1,2,0:T(8,128)(2,1)} %broadcast_in_dim.116), calls=%async_computation | async-start | bytes 4456448 | tf_op jit(solution)/shard_map/all_to_all | solution.py:22
  259.6 52.4 %all-to-all-done = bf16[8,256,544]{1,2,0:T(8,128)(2,1)} async-done(((bf16[8,256,544]{1,2,0:T(8,128)(2,1)}), bf16[8,256,544]{1,2,0:T(8,128)(2,1)}, u32[]{:S(2)}, u32[]{:S(2)}) %all-to-all-start) | async-done | bytes 2228256 | tf_op jit(solution)/shard_map/all_to_all | solution.py:22
  312.0 2.1 convert_reduce_fusion.2
  315.7 1.9 slice_negate_fusion.15
  343.5 2.9 multiply_multiply_fusion
  346.9 4.8 multiply_add_fusion.1
  357.6 2.2 pad.63
  359.8 2.2 pad.55
  363.5 2.2 pad.54
  370.3 2.1 pad.65
  373.4 2.1 pad.56
  375.5 2.1 pad.57
  378.8 2.8 add_multiply_fusion.1
  382.5 3.6 pad.59
  386.1 3.6 pad.128
  390.7 3.5 pad.66
  394.3 3.5 pad.87
  397.8 3.5 pad.58
  401.4 3.5 pad.126
  408.5 2.0 all_gather.24
  411.1 12.0 %all_gather.25 = bf16[4,16,1024]{2,1,0:T(8,128)(2,1)S(1)} all-gather(bf16[1,16,1024]{2,1,0:T(8,128)(2,1)S(1)} %get-tuple-element.872), channel_id=1, replica_groups=mesh['seq_0'=4,'seq_1'=4,'seq_2'=2,'mp'=8] {'seq_1'}, dimensions={0}, use_global_device_ids=true | all-gather | bytes 163840 | tf_op jit(solution)/shard_map/all_gather | solution.py:41
  423.1 12.0 %all_gather.28 = bf16[4,16,1024]{2,1,0:T(8,128)(2,1)S(1)} all-gather(bf16[1,16,1024]{2,1,0:T(8,128)(2,1)S(1)} %get-tuple-element.873), channel_id=1, replica_groups=mesh['seq_0'=4,'seq_1'=4,'seq_2'=2,'mp'=8] {'seq_1'}, dimensions={0}, use_global_device_ids=true | all-gather | bytes 163840 | tf_op jit(solution)/shard_map/all_gather | solution.py:41
  435.7 12.7 %all_gather.26 = bf16[4,16,1024]{2,1,0:T(8,128)(2,1)} all-gather(bf16[1,16,1024]{2,1,0:T(8,128)(2,1)S(1)} %get-tuple-element.850), channel_id=1, replica_groups=mesh['seq_0'=4,'seq_1'=4,'seq_2'=2,'mp'=8] {'seq_0'}, dimensions={0}, use_global_device_ids=true | all-gather | bytes 163840 | tf_op jit(solution)/shard_map/all_gather | solution.py:41
  448.5 12.7 %all_gather.29 = bf16[4,16,1024]{2,1,0:T(8,128)(2,1)} all-gather(bf16[1,16,1024]{2,1,0:T(8,128)(2,1)S(1)} %get-tuple-element.851), channel_id=1, replica_groups=mesh['seq_0'=4,'seq_1'=4,'seq_2'=2,'mp'=8] {'seq_0'}, dimensions={0}, use_global_device_ids=true | all-gather | bytes 163840 | tf_op jit(solution)/shard_map/all_gather | solution.py:41
  473.4 7.3 %multiply_add_fusion.2 = (f32[16,16,1024]{2,1,0:T(8,128)S(1)}, f32[16,16,1024]{2,1,0:T(8,128)S(1)}, f32[16,16,1024]{2,1,0:T(8,128)}, f32[16,16,1024]{2,1,0:T(8,1...) fusion(f32[16,16]{1,0:T(8,128)} %bitcast.283, ...), kind=kLoop, calls=%fused_computation.66 | loop fusion | flops 20185088 | bytes 12468160 | tf_op jit(solution)/shard_map/add | solution.py:148
  480.7 2.3 fusion.64
  492.4 2.9 multiply_reduce_fusion.3
  503.5 2.9 multiply_reduce_fusion.7
  514.7 2.6 multiply_reduce_fusion.11
  517.6 3.3 stack.67
  521.0 3.1 fusion.44
  (578 shorter events, 124.5 us)
Async XLA Ops:
  0.6 238.4 %copy-start = (bf16[1024,544]{0,1:T(8,128)(2,1)S(1)}, bf16[1024,544]{0,1:T(8,128)(2,1)}, u32[]{:S(2)}) copy-start(bf16[1024,544]{0,1:T(8,128)(2,1)} %param.24) | copy-start | bytes 3342340
  3.2 234.3 %collective-permute-start.2 = (bf16[3,1024]{1,0:T(4,128)(2,1)S(1)}, bf16[3,1024]{1,0:T(4,128)(2,1)S(1)}, u32[]{:S(2)}, u32[]{:S(2)}) collective-permute-start(bf16[3,1024]{1,0:T(4,128)(2,1)S(1)} %slice.545), channel_id=1, source_target_pairs={{0,8},{8,16},{16,24},{24,32},{32,40},{40,48},{48,56},{56,64},{64,7... | collective-permute-start | bytes 18440 | tf_op jit(solution)/shard_map/ppermute | solution.py:17
  13.9 7.6 %collective-permute-start = (bf16[256,128]{1,0:T(8,128)(2,1)S(1)}, bf16[256,128]{1,0:T(8,128)(2,1)S(1)}, u32[]{:S(2)}, u32[]{:S(2)}) collective-permute-start(bf16[256,128]{1,0:T(8,128)(2,1)S(1)} %get-tuple-element.1034), channel_id=1, source_target_pairs={{0,8},{8,16},{16,24},{24,32},{32,40},{40,48},{48,56},{56,64},{64,7... | collective-permute-start | bytes 196616 | tf_op jit(solution)/shard_map/while/body/eval_jaxpr/ppermute | solution.py:17
  17.6 3.9 collective-permute-start.1
  21.6 13.6 %collective-permute-start = (bf16[256,128]{1,0:T(8,128)(2,1)S(1)}, bf16[256,128]{1,0:T(8,128)(2,1)S(1)}, u32[]{:S(2)}, u32[]{:S(2)}) collective-permute-start(bf16[256,128]{1,0:T(8,128)(2,1)S(1)} %get-tuple-element.1034), channel_id=1, source_target_pairs={{0,8},{8,16},{16,24},{24,32},{32,40},{40,48},{48,56},{56,64},{64,7... | collective-permute-start | bytes 196616 | tf_op jit(solution)/shard_map/while/body/eval_jaxpr/ppermute | solution.py:17
  29.6 5.5 %collective-permute-start.1 = (bf16[256,128]{1,0:T(8,128)(2,1)S(1)}, bf16[256,128]{1,0:T(8,128)(2,1)S(1)}, u32[]{:S(2)}, u32[]{:S(2)}) collective-permute-start(bf16[256,128]{1,0:T(8,128)(2,1)S(1)} %get-tuple-element.1035), channel_id=1, source_target_pairs={{0,8},{8,16},{16,24},{24,32},{32,40},{40,48},{48,56},{56,64},{64,7... | collective-permute-start | bytes 196616 | tf_op jit(solution)/shard_map/while/body/eval_jaxpr/ppermute | solution.py:17
  35.3 11.9 %collective-permute-start = (bf16[256,128]{1,0:T(8,128)(2,1)S(1)}, bf16[256,128]{1,0:T(8,128)(2,1)S(1)}, u32[]{:S(2)}, u32[]{:S(2)}) collective-permute-start(bf16[256,128]{1,0:T(8,128)(2,1)S(1)} %get-tuple-element.1034), channel_id=1, source_target_pairs={{0,8},{8,16},{16,24},{24,32},{32,40},{40,48},{48,56},{56,64},{64,7... | collective-permute-start | bytes 196616 | tf_op jit(solution)/shard_map/while/body/eval_jaxpr/ppermute | solution.py:17
  37.2 10.0 %collective-permute-start.1 = (bf16[256,128]{1,0:T(8,128)(2,1)S(1)}, bf16[256,128]{1,0:T(8,128)(2,1)S(1)}, u32[]{:S(2)}, u32[]{:S(2)}) collective-permute-start(bf16[256,128]{1,0:T(8,128)(2,1)S(1)} %get-tuple-element.1035), channel_id=1, source_target_pairs={{0,8},{8,16},{16,24},{24,32},{32,40},{40,48},{48,56},{56,64},{64,7... | collective-permute-start | bytes 196616 | tf_op jit(solution)/shard_map/while/body/eval_jaxpr/ppermute | solution.py:17
  47.3 7.5 %collective-permute-start = (bf16[256,128]{1,0:T(8,128)(2,1)S(1)}, bf16[256,128]{1,0:T(8,128)(2,1)S(1)}, u32[]{:S(2)}, u32[]{:S(2)}) collective-permute-start(bf16[256,128]{1,0:T(8,128)(2,1)S(1)} %get-tuple-element.1034), channel_id=1, source_target_pairs={{0,8},{8,16},{16,24},{24,32},{32,40},{40,48},{48,56},{56,64},{64,7... | collective-permute-start | bytes 196616 | tf_op jit(solution)/shard_map/while/body/eval_jaxpr/ppermute | solution.py:17
  49.2 5.5 %collective-permute-start.1 = (bf16[256,128]{1,0:T(8,128)(2,1)S(1)}, bf16[256,128]{1,0:T(8,128)(2,1)S(1)}, u32[]{:S(2)}, u32[]{:S(2)}) collective-permute-start(bf16[256,128]{1,0:T(8,128)(2,1)S(1)} %get-tuple-element.1035), channel_id=1, source_target_pairs={{0,8},{8,16},{16,24},{24,32},{32,40},{40,48},{48,56},{56,64},{64,7... | collective-permute-start | bytes 196616 | tf_op jit(solution)/shard_map/while/body/eval_jaxpr/ppermute | solution.py:17
  54.8 13.2 %collective-permute-start = (bf16[256,128]{1,0:T(8,128)(2,1)S(1)}, bf16[256,128]{1,0:T(8,128)(2,1)S(1)}, u32[]{:S(2)}, u32[]{:S(2)}) collective-permute-start(bf16[256,128]{1,0:T(8,128)(2,1)S(1)} %get-tuple-element.1034), channel_id=1, source_target_pairs={{0,8},{8,16},{16,24},{24,32},{32,40},{40,48},{48,56},{56,64},{64,7... | collective-permute-start | bytes 196616 | tf_op jit(solution)/shard_map/while/body/eval_jaxpr/ppermute | solution.py:17
  60.9 7.2 %collective-permute-start.1 = (bf16[256,128]{1,0:T(8,128)(2,1)S(1)}, bf16[256,128]{1,0:T(8,128)(2,1)S(1)}, u32[]{:S(2)}, u32[]{:S(2)}) collective-permute-start(bf16[256,128]{1,0:T(8,128)(2,1)S(1)} %get-tuple-element.1035), channel_id=1, source_target_pairs={{0,8},{8,16},{16,24},{24,32},{32,40},{40,48},{48,56},{56,64},{64,7... | collective-permute-start | bytes 196616 | tf_op jit(solution)/shard_map/while/body/eval_jaxpr/ppermute | solution.py:17
  68.2 11.9 %collective-permute-start = (bf16[256,128]{1,0:T(8,128)(2,1)S(1)}, bf16[256,128]{1,0:T(8,128)(2,1)S(1)}, u32[]{:S(2)}, u32[]{:S(2)}) collective-permute-start(bf16[256,128]{1,0:T(8,128)(2,1)S(1)} %get-tuple-element.1034), channel_id=1, source_target_pairs={{0,8},{8,16},{16,24},{24,32},{32,40},{40,48},{48,56},{56,64},{64,7... | collective-permute-start | bytes 196616 | tf_op jit(solution)/shard_map/while/body/eval_jaxpr/ppermute | solution.py:17
  70.1 10.0 %collective-permute-start.1 = (bf16[256,128]{1,0:T(8,128)(2,1)S(1)}, bf16[256,128]{1,0:T(8,128)(2,1)S(1)}, u32[]{:S(2)}, u32[]{:S(2)}) collective-permute-start(bf16[256,128]{1,0:T(8,128)(2,1)S(1)} %get-tuple-element.1035), channel_id=1, source_target_pairs={{0,8},{8,16},{16,24},{24,32},{32,40},{40,48},{48,56},{56,64},{64,7... | collective-permute-start | bytes 196616 | tf_op jit(solution)/shard_map/while/body/eval_jaxpr/ppermute | solution.py:17
  80.2 7.5 %collective-permute-start = (bf16[256,128]{1,0:T(8,128)(2,1)S(1)}, bf16[256,128]{1,0:T(8,128)(2,1)S(1)}, u32[]{:S(2)}, u32[]{:S(2)}) collective-permute-start(bf16[256,128]{1,0:T(8,128)(2,1)S(1)} %get-tuple-element.1034), channel_id=1, source_target_pairs={{0,8},{8,16},{16,24},{24,32},{32,40},{40,48},{48,56},{56,64},{64,7... | collective-permute-start | bytes 196616 | tf_op jit(solution)/shard_map/while/body/eval_jaxpr/ppermute | solution.py:17
  82.1 5.5 %collective-permute-start.1 = (bf16[256,128]{1,0:T(8,128)(2,1)S(1)}, bf16[256,128]{1,0:T(8,128)(2,1)S(1)}, u32[]{:S(2)}, u32[]{:S(2)}) collective-permute-start(bf16[256,128]{1,0:T(8,128)(2,1)S(1)} %get-tuple-element.1035), channel_id=1, source_target_pairs={{0,8},{8,16},{16,24},{24,32},{32,40},{40,48},{48,56},{56,64},{64,7... | collective-permute-start | bytes 196616 | tf_op jit(solution)/shard_map/while/body/eval_jaxpr/ppermute | solution.py:17
  87.7 13.8 %collective-permute-start = (bf16[256,128]{1,0:T(8,128)(2,1)S(1)}, bf16[256,128]{1,0:T(8,128)(2,1)S(1)}, u32[]{:S(2)}, u32[]{:S(2)}) collective-permute-start(bf16[256,128]{1,0:T(8,128)(2,1)S(1)} %get-tuple-element.1034), channel_id=1, source_target_pairs={{0,8},{8,16},{16,24},{24,32},{32,40},{40,48},{48,56},{56,64},{64,7... | collective-permute-start | bytes 196616 | tf_op jit(solution)/shard_map/while/body/eval_jaxpr/ppermute | solution.py:17
  89.6 11.9 %collective-permute-start.1 = (bf16[256,128]{1,0:T(8,128)(2,1)S(1)}, bf16[256,128]{1,0:T(8,128)(2,1)S(1)}, u32[]{:S(2)}, u32[]{:S(2)}) collective-permute-start(bf16[256,128]{1,0:T(8,128)(2,1)S(1)} %get-tuple-element.1035), channel_id=1, source_target_pairs={{0,8},{8,16},{16,24},{24,32},{32,40},{40,48},{48,56},{56,64},{64,7... | collective-permute-start | bytes 196616 | tf_op jit(solution)/shard_map/while/body/eval_jaxpr/ppermute | solution.py:17
  101.6 9.6 %collective-permute-start = (bf16[256,128]{1,0:T(8,128)(2,1)S(1)}, bf16[256,128]{1,0:T(8,128)(2,1)S(1)}, u32[]{:S(2)}, u32[]{:S(2)}) collective-permute-start(bf16[256,128]{1,0:T(8,128)(2,1)S(1)} %get-tuple-element.1034), channel_id=1, source_target_pairs={{0,8},{8,16},{16,24},{24,32},{32,40},{40,48},{48,56},{56,64},{64,7... | collective-permute-start | bytes 196616 | tf_op jit(solution)/shard_map/while/body/eval_jaxpr/ppermute | solution.py:17
  103.5 7.6 %collective-permute-start.1 = (bf16[256,128]{1,0:T(8,128)(2,1)S(1)}, bf16[256,128]{1,0:T(8,128)(2,1)S(1)}, u32[]{:S(2)}, u32[]{:S(2)}) collective-permute-start(bf16[256,128]{1,0:T(8,128)(2,1)S(1)} %get-tuple-element.1035), channel_id=1, source_target_pairs={{0,8},{8,16},{16,24},{24,32},{32,40},{40,48},{48,56},{56,64},{64,7... | collective-permute-start | bytes 196616 | tf_op jit(solution)/shard_map/while/body/eval_jaxpr/ppermute | solution.py:17
  111.3 9.6 %collective-permute-start = (bf16[256,128]{1,0:T(8,128)(2,1)S(1)}, bf16[256,128]{1,0:T(8,128)(2,1)S(1)}, u32[]{:S(2)}, u32[]{:S(2)}) collective-permute-start(bf16[256,128]{1,0:T(8,128)(2,1)S(1)} %get-tuple-element.1034), channel_id=1, source_target_pairs={{0,8},{8,16},{16,24},{24,32},{32,40},{40,48},{48,56},{56,64},{64,7... | collective-permute-start | bytes 196616 | tf_op jit(solution)/shard_map/while/body/eval_jaxpr/ppermute | solution.py:17
  113.2 7.6 %collective-permute-start.1 = (bf16[256,128]{1,0:T(8,128)(2,1)S(1)}, bf16[256,128]{1,0:T(8,128)(2,1)S(1)}, u32[]{:S(2)}, u32[]{:S(2)}) collective-permute-start(bf16[256,128]{1,0:T(8,128)(2,1)S(1)} %get-tuple-element.1035), channel_id=1, source_target_pairs={{0,8},{8,16},{16,24},{24,32},{32,40},{40,48},{48,56},{56,64},{64,7... | collective-permute-start | bytes 196616 | tf_op jit(solution)/shard_map/while/body/eval_jaxpr/ppermute | solution.py:17
  120.9 9.6 %collective-permute-start = (bf16[256,128]{1,0:T(8,128)(2,1)S(1)}, bf16[256,128]{1,0:T(8,128)(2,1)S(1)}, u32[]{:S(2)}, u32[]{:S(2)}) collective-permute-start(bf16[256,128]{1,0:T(8,128)(2,1)S(1)} %get-tuple-element.1034), channel_id=1, source_target_pairs={{0,8},{8,16},{16,24},{24,32},{32,40},{40,48},{48,56},{56,64},{64,7... | collective-permute-start | bytes 196616 | tf_op jit(solution)/shard_map/while/body/eval_jaxpr/ppermute | solution.py:17
  122.9 7.6 %collective-permute-start.1 = (bf16[256,128]{1,0:T(8,128)(2,1)S(1)}, bf16[256,128]{1,0:T(8,128)(2,1)S(1)}, u32[]{:S(2)}, u32[]{:S(2)}) collective-permute-start(bf16[256,128]{1,0:T(8,128)(2,1)S(1)} %get-tuple-element.1035), channel_id=1, source_target_pairs={{0,8},{8,16},{16,24},{24,32},{32,40},{40,48},{48,56},{56,64},{64,7... | collective-permute-start | bytes 196616 | tf_op jit(solution)/shard_map/while/body/eval_jaxpr/ppermute | solution.py:17
  130.6 9.6 %collective-permute-start = (bf16[256,128]{1,0:T(8,128)(2,1)S(1)}, bf16[256,128]{1,0:T(8,128)(2,1)S(1)}, u32[]{:S(2)}, u32[]{:S(2)}) collective-permute-start(bf16[256,128]{1,0:T(8,128)(2,1)S(1)} %get-tuple-element.1034), channel_id=1, source_target_pairs={{0,8},{8,16},{16,24},{24,32},{32,40},{40,48},{48,56},{56,64},{64,7... | collective-permute-start | bytes 196616 | tf_op jit(solution)/shard_map/while/body/eval_jaxpr/ppermute | solution.py:17
  132.5 7.6 %collective-permute-start.1 = (bf16[256,128]{1,0:T(8,128)(2,1)S(1)}, bf16[256,128]{1,0:T(8,128)(2,1)S(1)}, u32[]{:S(2)}, u32[]{:S(2)}) collective-permute-start(bf16[256,128]{1,0:T(8,128)(2,1)S(1)} %get-tuple-element.1035), channel_id=1, source_target_pairs={{0,8},{8,16},{16,24},{24,32},{32,40},{40,48},{48,56},{56,64},{64,7... | collective-permute-start | bytes 196616 | tf_op jit(solution)/shard_map/while/body/eval_jaxpr/ppermute | solution.py:17
  140.3 13.7 %collective-permute-start = (bf16[256,128]{1,0:T(8,128)(2,1)S(1)}, bf16[256,128]{1,0:T(8,128)(2,1)S(1)}, u32[]{:S(2)}, u32[]{:S(2)}) collective-permute-start(bf16[256,128]{1,0:T(8,128)(2,1)S(1)} %get-tuple-element.1034), channel_id=1, source_target_pairs={{0,8},{8,16},{16,24},{24,32},{32,40},{40,48},{48,56},{56,64},{64,7... | collective-permute-start | bytes 196616 | tf_op jit(solution)/shard_map/while/body/eval_jaxpr/ppermute | solution.py:17
  146.3 7.7 %collective-permute-start.1 = (bf16[256,128]{1,0:T(8,128)(2,1)S(1)}, bf16[256,128]{1,0:T(8,128)(2,1)S(1)}, u32[]{:S(2)}, u32[]{:S(2)}) collective-permute-start(bf16[256,128]{1,0:T(8,128)(2,1)S(1)} %get-tuple-element.1035), channel_id=1, source_target_pairs={{0,8},{8,16},{16,24},{24,32},{32,40},{40,48},{48,56},{56,64},{64,7... | collective-permute-start | bytes 196616 | tf_op jit(solution)/shard_map/while/body/eval_jaxpr/ppermute | solution.py:17
  154.1 14.0 %collective-permute-start = (bf16[256,128]{1,0:T(8,128)(2,1)S(1)}, bf16[256,128]{1,0:T(8,128)(2,1)S(1)}, u32[]{:S(2)}, u32[]{:S(2)}) collective-permute-start(bf16[256,128]{1,0:T(8,128)(2,1)S(1)} %get-tuple-element.1034), channel_id=1, source_target_pairs={{0,8},{8,16},{16,24},{24,32},{32,40},{40,48},{48,56},{56,64},{64,7... | collective-permute-start | bytes 196616 | tf_op jit(solution)/shard_map/while/body/eval_jaxpr/ppermute | solution.py:17
  156.0 12.1 %collective-permute-start.1 = (bf16[256,128]{1,0:T(8,128)(2,1)S(1)}, bf16[256,128]{1,0:T(8,128)(2,1)S(1)}, u32[]{:S(2)}, u32[]{:S(2)}) collective-permute-start(bf16[256,128]{1,0:T(8,128)(2,1)S(1)} %get-tuple-element.1035), channel_id=1, source_target_pairs={{0,8},{8,16},{16,24},{24,32},{32,40},{40,48},{48,56},{56,64},{64,7... | collective-permute-start | bytes 196616 | tf_op jit(solution)/shard_map/while/body/eval_jaxpr/ppermute | solution.py:17
  168.2 9.6 %collective-permute-start = (bf16[256,128]{1,0:T(8,128)(2,1)S(1)}, bf16[256,128]{1,0:T(8,128)(2,1)S(1)}, u32[]{:S(2)}, u32[]{:S(2)}) collective-permute-start(bf16[256,128]{1,0:T(8,128)(2,1)S(1)} %get-tuple-element.1034), channel_id=1, source_target_pairs={{0,8},{8,16},{16,24},{24,32},{32,40},{40,48},{48,56},{56,64},{64,7... | collective-permute-start | bytes 196616 | tf_op jit(solution)/shard_map/while/body/eval_jaxpr/ppermute | solution.py:17
  170.1 7.7 %collective-permute-start.1 = (bf16[256,128]{1,0:T(8,128)(2,1)S(1)}, bf16[256,128]{1,0:T(8,128)(2,1)S(1)}, u32[]{:S(2)}, u32[]{:S(2)}) collective-permute-start(bf16[256,128]{1,0:T(8,128)(2,1)S(1)} %get-tuple-element.1035), channel_id=1, source_target_pairs={{0,8},{8,16},{16,24},{24,32},{32,40},{40,48},{48,56},{56,64},{64,7... | collective-permute-start | bytes 196616 | tf_op jit(solution)/shard_map/while/body/eval_jaxpr/ppermute | solution.py:17
  177.8 14.0 %collective-permute-start = (bf16[256,128]{1,0:T(8,128)(2,1)S(1)}, bf16[256,128]{1,0:T(8,128)(2,1)S(1)}, u32[]{:S(2)}, u32[]{:S(2)}) collective-permute-start(bf16[256,128]{1,0:T(8,128)(2,1)S(1)} %get-tuple-element.1034), channel_id=1, source_target_pairs={{0,8},{8,16},{16,24},{24,32},{32,40},{40,48},{48,56},{56,64},{64,7... | collective-permute-start | bytes 196616 | tf_op jit(solution)/shard_map/while/body/eval_jaxpr/ppermute | solution.py:17
  184.2 7.7 %collective-permute-start.1 = (bf16[256,128]{1,0:T(8,128)(2,1)S(1)}, bf16[256,128]{1,0:T(8,128)(2,1)S(1)}, u32[]{:S(2)}, u32[]{:S(2)}) collective-permute-start(bf16[256,128]{1,0:T(8,128)(2,1)S(1)} %get-tuple-element.1035), channel_id=1, source_target_pairs={{0,8},{8,16},{16,24},{24,32},{32,40},{40,48},{48,56},{56,64},{64,7... | collective-permute-start | bytes 196616 | tf_op jit(solution)/shard_map/while/body/eval_jaxpr/ppermute | solution.py:17
  192.3 45.0 %copy-start.123 = (f32[4,1024]{1,0:T(4,128)S(1)}, f32[4,1024]{1,0:T(4,128)}, u32[]{:S(2)}) copy-start(f32[4,1024]{1,0:T(4,128)} %param.22) | copy-start | bytes 49156
  192.3 45.1 %copy-start.55 = (bf16[256,1024]{1,0:T(8,128)(2,1)S(1)}, bf16[256,1024]{1,0:T(8,128)(2,1)}, u32[]{:S(2)}) copy-start(bf16[256,1024]{1,0:T(8,128)(2,1)} %param.20) | copy-start | bytes 1572868
  192.9 45.1 %copy-start.124 = (f32[1024]{0:T(1024)S(1)}, f32[1024]{0:T(1024)}, u32[]{:S(2)}) copy-start(f32[1024]{0:T(1024)} %param.23) | copy-start | bytes 12292
  196.9 51.3 %all-to-all-start.1 = ((bf16[32,8,1024]{2,1,0:T(8,128)(2,1)}), bf16[32,8,1024]{2,1,0:T(8,128)(2,1)S(1)}, u32[]{:S(2)}, u32[]{:S(2)}) async-start(bf16[32,8,1024]{2,1,0:T(8,128)(2,1)} %gather_fusion), calls=%async_computation.1 | async-start | bytes 1048576 | tf_op jit(solution)/shard_map/all_to_all | solution.py:264
  249.8 62.2 %all-to-all-start = ((bf16[8,256,544]{1,2,0:T(8,128)(2,1)}), bf16[8,256,544]{1,2,0:T(8,128)(2,1)}, u32[]{:S(2)}, u32[]{:S(2)}) async-start(bf16[8,256,544]{1,2,0:T(8,128)(2,1)} %broadcast_in_dim.116), calls=%async_computation | async-start | bytes 4456448 | tf_op jit(solution)/shard_map/all_to_all | solution.py:22
  258.4 56.3 %copy-start.152 = (f32[1024]{0:T(1024)S(1)}, f32[1024]{0:T(1024)}, u32[]{:S(2)}) copy-start(f32[1024]{0:T(1024)} %param.26) | copy-start | bytes 12292
  329.6 13.4 %copy-start.94 = (f32[16,1,1024]{2,1,0:T(1,128)S(1)}, f32[16,1,1024]{2,1,0:T(1,128)}, u32[]{:S(2)}) copy-start(f32[16,1,1024]{2,1,0:T(1,128)} %get-tuple-element.801) | copy-start | bytes 196612
  329.6 13.4 %copy-start.95 = (f32[16,1,1024]{2,1,0:T(1,128)S(1)}, f32[16,1,1024]{2,1,0:T(1,128)}, u32[]{:S(2)}) copy-start(f32[16,1,1024]{2,1,0:T(1,128)} %get-tuple-element.802) | copy-start | bytes 196612
  330.4 12.7 %copy-start.100 = (f32[16,1,1024]{2,1,0:T(1,128)S(1)}, f32[16,1,1024]{2,1,0:T(1,128)}, u32[]{:S(2)}) copy-start(f32[16,1,1024]{2,1,0:T(1,128)} %get-tuple-element.810) | copy-start | bytes 196612
  330.4 12.7 %copy-start.101 = (f32[16,1,1024]{2,1,0:T(1,128)S(1)}, f32[16,1,1024]{2,1,0:T(1,128)}, u32[]{:S(2)}) copy-start(f32[16,1,1024]{2,1,0:T(1,128)} %get-tuple-element.811) | copy-start | bytes 196612
  331.3 15.1 %copy-start.118 = (f32[16,1,16]{2,0,1:T(8,128)}, f32[16,1,16]{2,0,1:T(8,128)S(1)}, u32[]{:S(2)}) copy-start(f32[16,1,16]{2,0,1:T(8,128)S(1)} %copy.124) | copy-start | bytes 3076
  331.3 11.8 %copy-start.92 = (f32[16,1,1024]{2,1,0:T(1,128)S(1)}, f32[16,1,1024]{2,1,0:T(1,128)}, u32[]{:S(2)}) copy-start(f32[16,1,1024]{2,1,0:T(1,128)} %get-tuple-element.803) | copy-start | bytes 196612
  331.3 11.8 %copy-start.93 = (f32[16,1,1024]{2,1,0:T(1,128)S(1)}, f32[16,1,1024]{2,1,0:T(1,128)}, u32[]{:S(2)}) copy-start(f32[16,1,1024]{2,1,0:T(1,128)} %get-tuple-element.804) | copy-start | bytes 196612
  331.5 14.9 %copy-start.119 = (f32[16,1,16]{2,0,1:T(8,128)}, f32[16,1,16]{2,0,1:T(8,128)S(1)}, u32[]{:S(2)}) copy-start(f32[16,1,16]{2,0,1:T(8,128)S(1)} %copy.126) | copy-start | bytes 3076
  331.7 14.8 %copy-start.120 = (f32[16,1,16]{2,0,1:T(8,128)}, f32[16,1,16]{2,0,1:T(8,128)S(1)}, u32[]{:S(2)}) copy-start(f32[16,1,16]{2,0,1:T(8,128)S(1)} %copy.128) | copy-start | bytes 3076
  331.7 11.5 %copy-start.99 = (f32[16,1,1024]{2,1,0:T(1,128)S(1)}, f32[16,1,1024]{2,1,0:T(1,128)}, u32[]{:S(2)}) copy-start(f32[16,1,1024]{2,1,0:T(1,128)} %get-tuple-element.809) | copy-start | bytes 196612
  331.9 14.6 %copy-start.121 = (f32[16,1,16]{2,0,1:T(8,128)}, f32[16,1,16]{2,0,1:T(8,128)S(1)}, u32[]{:S(2)}) copy-start(f32[16,1,16]{2,0,1:T(8,128)S(1)} %copy.130) | copy-start | bytes 3076
  332.1 14.4 %copy-start.122 = (f32[16,1,16]{2,0,1:T(8,128)}, f32[16,1,16]{2,0,1:T(8,128)S(1)}, u32[]{:S(2)}) copy-start(f32[16,1,16]{2,0,1:T(8,128)S(1)} %copy.132) | copy-start | bytes 3076
  332.2 14.3 %copy-start.114 = (f32[16,1,16]{2,0,1:T(8,128)}, f32[16,1,16]{2,0,1:T(8,128)S(1)}, u32[]{:S(2)}) copy-start(f32[16,1,16]{2,0,1:T(8,128)S(1)} %copy.133) | copy-start | bytes 3076
  333.3 13.2 %copy-start.58 = (f32[16,1024]{1,0:T(8,128)}, f32[16,1024]{1,0:T(8,128)S(1)}, u32[]{:S(2)}) copy-start(f32[16,1024]{1,0:T(8,128)S(1)} %get-tuple-element.915) | copy-start | bytes 196612
  333.3 13.2 %copy-start.90 = (f32[16,1024]{1,0:T(8,128)}, f32[16,1024]{1,0:T(8,128)S(1)}, u32[]{:S(2)}) copy-start(f32[16,1024]{1,0:T(8,128)S(1)} %get-tuple-element.914) | copy-start | bytes 196612
  334.3 12.3 %copy-start.19 = (f32[16,1024]{1,0:T(8,128)}, f32[16,1024]{1,0:T(8,128)S(1)}, u32[]{:S(2)}) copy-start(f32[16,1024]{1,0:T(8,128)S(1)} %get-tuple-element.900) | copy-start | bytes 196612
  334.3 12.3 %copy-start.60 = (f32[16,1024]{1,0:T(8,128)}, f32[16,1024]{1,0:T(8,128)S(1)}, u32[]{:S(2)}) copy-start(f32[16,1024]{1,0:T(8,128)S(1)} %get-tuple-element.901) | copy-start | bytes 196612
  404.9 56.3 %copy-start.4 = (f32[15,16,1024]{2,1,0:T(8,128)S(1)}, f32[15,16,1024]{2,1,0:T(8,128)}, u32[]{:S(2)}) copy-start(f32[15,16,1024]{2,1,0:T(8,128)} %pad.87) | copy-start | bytes 2949124
  408.5 53.8 %copy-start.105 = (f32[256,16]{0,1:T(8,128)S(1)}, f32[256,16]{0,1:T(8,128)}, u32[]{:S(2)}) copy-start(f32[256,16]{0,1:T(8,128)} %get-tuple-element.822) | copy-start | bytes 49156
  423.1 12.0 %copy-start.14 = (bf16[4,16,1024]{2,1,0:T(8,128)(2,1)}, bf16[4,16,1024]{2,1,0:T(8,128)(2,1)S(1)}, u32[]{:S(2)}) copy-start(bf16[4,16,1024]{2,1,0:T(8,128)(2,1)S(1)} %all_gather.25) | copy-start | bytes 393220
  480.7 11.7 %copy-start.39 = (f32[16,1024]{1,0:T(8,128)S(1)}, f32[16,1024]{1,0:T(8,128)}, u32[]{:S(2)}) copy-start(f32[16,1024]{1,0:T(8,128)} %copy-done.37) | copy-start | bytes 196612
  480.7 11.7 %copy-start.42 = (f32[16,1024]{1,0:T(8,128)S(1)}, f32[16,1024]{1,0:T(8,128)}, u32[]{:S(2)}) copy-start(f32[16,1024]{1,0:T(8,128)} %copy-done.40) | copy-start | bytes 196612
  500.2 14.5 %copy-start.23 = (f32[16,1024]{1,0:T(8,128)S(1)}, f32[16,1024]{1,0:T(8,128)}, u32[]{:S(2)}) copy-start(f32[16,1024]{1,0:T(8,128)} %copy-done.21) | copy-start | bytes 196612
  500.2 14.5 %copy-start.26 = (f32[16,1024]{1,0:T(8,128)S(1)}, f32[16,1024]{1,0:T(8,128)}, u32[]{:S(2)}) copy-start(f32[16,1024]{1,0:T(8,128)} %copy-done.24) | copy-start | bytes 196612
  (127 other events, 640.5 us)
where the time goes:
time: 531 us; the launch traced here: 525 us
  starting transfers between devices  196 us (37%)
  local copies, waits for them, and re-layouts  115 us (22%)
  other arithmetic  70.2 us (13%)
  waiting for transfers between devices  61.2 us (12%)
  blocking collectives  53.2 us (10%)
  loops' own time  22.1 us (4%)
    ppermute x33, starting transfers between devices, shifted_2(): lax.ppermute(value, axis, [(source, source + steps) for source in range(f...  147 us
    all_gather x6, blocking collectives, entering(): lax.all_gather(part.astype(kind), axis)  53.2 us
    all_to_all x1, waiting for transfers between devices, sent_to_all(): return lax.all_to_all(copies, axis, split_axis=0, concat_axis=0, tiled=True)  52.4 us
    all_to_all x1, starting transfers between devices, attention_mixer(): lax.all_to_all(outgoing, SEQ, split_axis=0, concat_axis=0, tiled=True)  40.3 us
    slice x17, local copies, waits for them, and re-layouts, mamba_mixer(): outputs.append(jnp.sum(c_blocks[:, offset, :, None] * carried, axis=1))  26.2 us
    unnamed x331, local copies, waits for them, and re-layouts  25.4 us
    pad x11, local copies, waits for them, and re-layouts, mamba_mixer(): inclusive = lax.associative_scan(chain_states, (decayed, carried), axis=0)  24.5 us
    another operation x1, loops' own time, attention_mixer(): lax.fori_loop(1, reach_count + 1, look_back, (carried, (key_rows, value_r...  21.8 us
  transfers between devices with their start and end apart: 35, of which 2 were waited for; matrix products, arithmetic and copies ran while one was open for 5% of the time, Pallas kernels for 0%

commit v1 on v0

v1 whole, which is shorter than its diff:
```python
import math

import jax
import jax.numpy as jnp
from jax import lax
from jax.experimental import pallas as pl
from jax.experimental.pallas import tpu as pltpu
from jax.sharding import Mesh
from jax.sharding import PartitionSpec as P

SEQ = ("seq_0", "seq_1", "seq_2")
MESH = pl.DeviceIdType.MESH
VM = pltpu.VMEM
F32 = jnp.float32
BF16 = jnp.bfloat16
LOG2E = math.log2(math.e)
NX, NY, NC, NZ = 4, 4, 2, 8
NSEQ = NX * NY * NC
TOK = 256
CH = 1024
LANE = 128
SUB = CH // LANE
NS = 16
RANK = 512
PROJ = RANK + 2 * NS
HD = 128
TAPS = 4
REACH = 16
BIG_STEP = 1.0e7
MASKED = -1.0e30
GROUP = 4
RUN = TOK // NSEQ
BK = 256
VLIM = 60 * 1024 * 1024


def whole(space=VM):
    return pl.BlockSpec(memory_space=space)


def place():
    return (
        lax.axis_index("seq_0"),
        lax.axis_index("seq_1"),
        lax.axis_index("seq_2"),
        lax.axis_index("mp"),
    )


def seq_device(j, z):
    return (j // (NY * NC), (j // NC) % NY, j % NC, z)


def doc_starts(len_ref):
    s1 = len_ref[0]
    s2 = s1 + len_ref[1]
    return s1, s2, s2 + len_ref[2]


def start_of(pos, starts):
    s1, s2, s3 = starts
    return jnp.where(pos >= s3, s3, jnp.where(pos >= s2, s2, jnp.where(pos >= s1, s1, 0)))


def silu(x):
    return x / (1.0 + jnp.exp(-x))


def gather_kernel(
    inv_ref,
    len_ref,
    q_ref,
    k_ref,
    v_ref,
    x_ref,
    cw_ref,
    cb_ref,
    xw_ref,
    q_out,
    kv_out,
    proj_out,
    inner_out,
    kvs,
    qs,
    halo,
    ext,
    part,
    rs,
    own,
    loc_sem,
    halo_sem,
    kv_send,
    kv_recv,
    q_send,
    q_recv,
    rs_send,
    rs_recv,
    ag_send,
    ag_recv,
):
    x, y, c, z = place()
    me = (x * NY + y) * NC + c
    barrier = pltpu.get_barrier_semaphore()
    for k in range(1, NSEQ):
        pl.semaphore_signal(
            barrier, inc=1, device_id=seq_device((me + k) % NSEQ, z), device_id_type=MESH
        )
    for k in range(1, NZ):
        pl.semaphore_signal(
            barrier, inc=1, device_id=(x, y, c, (z + k) % NZ), device_id_type=MESH
        )
    load_k = pltpu.make_async_copy(k_ref, kvs.at[:, pl.ds(0, HD)], loc_sem.at[0])
    load_v = pltpu.make_async_copy(v_ref, kvs.at[:, pl.ds(HD, HD)], loc_sem.at[1])
    load_k.start()
    load_v.start()
    for j in range(NSEQ):
        qs[j] = q_ref[inv_ref[j]]
    load_k.wait()
    load_v.wait()
    pl.semaphore_wait(barrier, NSEQ - 1 + NZ - 1)

    def remote(src, dst, send, recv, device):
        return pltpu.make_async_remote_copy(
            src_ref=src,
            dst_ref=dst,
            send_sem=send,
            recv_sem=recv,
            device_id=device,
            device_id_type=MESH,
        )

    def offset(a, b, core):
        return (x + a * (1 - core) + b * core) % NX, (y + a * core + b * (1 - core)) % NY

    def rows_of(a, b, core):
        px, py = offset(a, b, core)
        return pl.ds(pl.multiple_of(((px * NY + py) * NC + core) * TOK, TOK), TOK)

    partner = (x, y, 1 - c, z)
    after = (me + 1) % NSEQ
    halo_copy = remote(
        x_ref.at[pl.ds(TOK - 16, 16)], halo, halo_sem.at[0], halo_sem.at[1], seq_device(after, z)
    )
    halo_copy.start()
    mine = kv_out.at[rows_of(0, 0, c)]
    sends = []
    for a in range(1, NX):
        px, py = offset(a, 0, c)
        copy = remote(kvs, mine, kv_send.at[a], kv_recv.at[a], (px, py, c, z))
        copy.start()
        sends.append(copy)
    copy = remote(kvs, mine, kv_send.at[16], kv_recv.at[16], partner)
    copy.start()
    sends.append(copy)
    keep_kv = pltpu.make_async_copy(kvs, mine, loc_sem.at[0])
    keep_kv.start()
    q_rows = pl.ds(pl.multiple_of(me * RUN, RUN), RUN)
    for k in range(1, NSEQ):
        j = (me + k) % NSEQ
        copy = remote(qs.at[j], q_out.at[q_rows], q_send.at[k], q_recv.at[k], seq_device(j, z))
        copy.start()
        sends.append(copy)
    keep_q = pltpu.make_async_copy(qs.at[me], q_out.at[q_rows], loc_sem.at[1])
    keep_q.start()

    halo_copy.wait()
    ext[pl.ds(0, 8), :] = halo[pl.ds(8, 8), :].astype(F32)
    starts = doc_starts(len_ref)
    token = me * TOK + lax.broadcasted_iota(jnp.int32, (TOK, LANE), 0)
    depth = token - start_of(token, starts)

    def conv_columns(i, carry):
        cols = pl.ds(pl.multiple_of(i * LANE, LANE), LANE)
        ext[pl.ds(8, TOK), cols] = x_ref[:, cols].astype(F32)
        total = cb_ref[:, cols] + cw_ref[pl.ds(0, 1), cols] * ext[pl.ds(8, TOK), cols]
        for lag in range(1, TAPS):
            window = ext[pl.ds(8 - lag, TOK), cols]
            total = total + cw_ref[pl.ds(lag, 1), cols] * jnp.where(depth >= lag, window, 0.0)
        inner_out[:, cols] = silu(total).astype(BF16)
        return carry

    lax.fori_loop(0, SUB, conv_columns, 0)

    partial = jnp.dot(inner_out[...], xw_ref[...], preferred_element_type=F32).astype(BF16)
    part[...] = partial.reshape(NZ, TOK // NZ, PROJ)
    for k in range(1, NZ):
        j = (z + k) % NZ
        copy = remote(part.at[j], rs.at[k], rs_send.at[k], rs_recv.at[k], (x, y, c, j))
        copy.start()
        sends.append(copy)

    def wait_kv(slot_rows, index):
        remote(kvs, kv_out.at[slot_rows], kv_send.at[0], kv_recv.at[index], partner).wait_recv()

    for a in range(NX):
        if a > 0:
            wait_kv(rows_of(-a, 0, c), a)
        block = kv_out.at[rows_of(-a, 0, c)] if a > 0 else kvs
        target = kv_out.at[rows_of(-a, 0, c)]
        for b in range(1, NY):
            px, py = offset(0, b, c)
            index = b * NX + a
            copy = remote(block, target, kv_send.at[index], kv_recv.at[index], (px, py, c, z))
            copy.start()
            sends.append(copy)
        if a > 0:
            copy = remote(block, target, kv_send.at[16 + a], kv_recv.at[16 + a], partner)
            copy.start()
            sends.append(copy)

    total = part[z].astype(F32)
    for k in range(1, NZ):
        remote(part.at[0], rs.at[k], rs_send.at[k], rs_recv.at[k], partner).wait_recv()
        total = total + rs[k].astype(F32)
    own[...] = total.astype(BF16)
    slice_rows = TOK // NZ
    own_rows = pl.ds(pl.multiple_of(z * slice_rows, slice_rows), slice_rows)
    for k in range(1, NZ):
        copy = remote(
            own, proj_out.at[own_rows], ag_send.at[k], ag_recv.at[k], (x, y, c, (z + k) % NZ)
        )
        copy.start()
        sends.append(copy)
    proj_out[own_rows, :] = own[...]

    for b in range(1, NY):
        for a in range(NX):
            index = b * NX + a
            wait_kv(rows_of(-a, -b, c), index)
            block = kv_out.at[rows_of(-a, -b, c)]
            copy = remote(block, block, kv_send.at[16 + index], kv_recv.at[16 + index], partner)
            copy.start()
            sends.append(copy)
    for k in range(1, NZ):
        rows = pl.ds(pl.multiple_of(((z + NZ - k) % NZ) * slice_rows, slice_rows), slice_rows)
        remote(own, proj_out.at[rows], ag_send.at[k], ag_recv.at[k], partner).wait_recv()
    for k in range(1, NSEQ):
        rows = pl.ds(pl.multiple_of(((me + NSEQ - k) % NSEQ) * RUN, RUN), RUN)
        remote(qs.at[0], q_out.at[rows], q_send.at[k], q_recv.at[k], partner).wait_recv()
    for b in range(NY):
        for a in range(NX):
            wait_kv(rows_of(-a, -b, 1 - c), 16 + b * NX + a)
    for copy in sends:
        copy.wait_send()
    keep_kv.wait()
    keep_q.wait()


def gather_all(inverse, lengths, q, k, v, x, cw, cb, xw):
    dma = pltpu.SemaphoreType.DMA
    return pl.pallas_call(
        gather_kernel,
        out_shape=(
            jax.ShapeDtypeStruct((TOK, CH), BF16),
            jax.ShapeDtypeStruct((NSEQ * TOK, 2 * HD), BF16),
            jax.ShapeDtypeStruct((TOK, PROJ), BF16),
            jax.ShapeDtypeStruct((TOK, CH), BF16),
        ),
        in_specs=[whole(pltpu.SMEM)] * 2
        + [whole()]
        + [whole(pl.ANY)] * 2
        + [whole()] * 4,
        out_specs=(whole(pl.ANY), whole(pl.ANY), whole(), whole()),
        scratch_shapes=[
            VM((TOK, 2 * HD), BF16),
            VM((NSEQ, RUN, CH), BF16),
            VM((16, CH), BF16),
            VM((TOK + 8, CH), F32),
            VM((NZ, TOK // NZ, PROJ), BF16),
            VM((NZ, TOK // NZ, PROJ), BF16),
            VM((TOK // NZ, PROJ), BF16),
            dma((2,)),
            dma((2,)),
            dma((32,)),
            dma((32,)),
            dma((NSEQ,)),
            dma((NSEQ,)),
            dma((NZ,)),
            dma((NZ,)),
            dma((NZ,)),
            dma((NZ,)),
        ],
        compiler_params=pltpu.CompilerParams(
            collective_id=0, has_side_effects=True, vmem_limit_bytes=VLIM
        ),
        name="gather",
    )(inverse, lengths, q, k, v, x, cw, cb, xw)


def spread_columns(proj_ref, first, count):
    row = lax.broadcasted_iota(jnp.int32, (count, count * LANE), 0)
    col = lax.broadcasted_iota(jnp.int32, (count, count * LANE), 1)
    pick = jnp.where(col // LANE == row, 1.0, 0.0).astype(BF16)
    return jnp.dot(proj_ref[:, pl.ds(first, count)], pick, preferred_element_type=F32)


def local_scan_kernel(
    len_ref, me_ref, proj_ref, inner_ref, dtw_ref, dtb_ref, rate_ref, st_out, step_out, drive_out,
    rate_out, bcs, sums,
):
    starts = doc_starts(len_ref)
    token = me_ref[0] * TOK + lax.broadcasted_iota(jnp.int32, (TOK, LANE), 0)
    begins = token == start_of(token, starts)
    for j in range(SUB):
        cols = pl.ds(j * LANE, LANE)
        raw = jnp.dot(proj_ref[:, pl.ds(0, RANK)], dtw_ref[:, cols], preferred_element_type=F32)
        step = jax.nn.softplus(raw + dtb_ref[:, cols])
        drive = step * inner_ref[:, cols].astype(F32)
        step = jnp.where(begins, BIG_STEP, step)
        sums[pl.ds(j, 1), :] = jnp.sum(step, axis=0, keepdims=True)
        step_out[pl.ds(j, TOK, stride=SUB), :] = step
        drive_out[pl.ds(j, TOK, stride=SUB), :] = drive
        rate_out[pl.ds(j, NS, stride=SUB), :] = rate_ref[:, cols] * (-LOG2E)
    spread = spread_columns(proj_ref, RANK, NS)
    for n in range(NS):
        bcs[pl.ds(n * TOK, TOK), :] = spread[:, n * LANE : (n + 1) * LANE]
    rates = [rate_out[pl.ds(n * SUB, SUB), :] for n in range(NS)]

    def advance(t, carried):
        rows = pl.ds(pl.multiple_of(t * SUB, SUB), SUB)
        step = step_out[rows, :]
        drive = drive_out[rows, :]
        result = []
        for n in range(NS):
            b = bcs[pl.ds(n * TOK + t, SUB, stride=0), :]
            result.append(jnp.exp2(step * rates[n]) * carried[n] + b * drive)
        return tuple(result)

    zero = jnp.zeros((SUB, LANE), F32)
    state = lax.fori_loop(0, TOK, advance, (zero,) * NS, unroll=4)
    for n in range(0, NS, 2):
        pair = jnp.concatenate([state[n], state[n + 1]], axis=0)
        st_out[pl.ds(n * SUB, 2 * SUB), :] = pair.astype(BF16)
    total = sums[...]
    high = total.astype(BF16)
    low = total - high.astype(F32)
    st_out[pl.ds(NS * SUB, 2 * SUB), :] = jnp.concatenate([high.astype(F32), low], axis=0).astype(BF16)


def local_scan(lengths, me, proj, inner, dtw, dtb, rate):
    return pl.pallas_call(
        local_scan_kernel,
        out_shape=(
            jax.ShapeDtypeStruct(((NS + 2) * SUB, LANE), BF16),
            jax.ShapeDtypeStruct((TOK * SUB, LANE), F32),
            jax.ShapeDtypeStruct((TOK * SUB, LANE), F32),
            jax.ShapeDtypeStruct((NS * SUB, LANE), F32),
        ),
        in_specs=[whole(pltpu.SMEM)] * 2 + [whole()] * 5,
        out_specs=(whole(),) * 4,
        scratch_shapes=[VM((NS * TOK, LANE), F32), VM((SUB, LANE), F32)],
        compiler_params=pltpu.CompilerParams(vmem_limit_bytes=VLIM),
        name="local_scan",
    )(lengths, me, proj, inner, dtw, dtb, rate)


def enter_kernel(st_ref, rate_ref, in_out, slots, send_sem, recv_sem):
    x, y, c, z = place()
    me = (x * NY + y) * NC + c
    barrier = pltpu.get_barrier_semaphore()
    for k in range(1, REACH + 1):
        pl.semaphore_signal(
            barrier, inc=1, device_id=seq_device((me + NSEQ - k) % NSEQ, z), device_id_type=MESH
        )
    pl.semaphore_wait(barrier, REACH)
    copies = []
    for k in range(1, REACH + 1):
        copy = pltpu.make_async_remote_copy(
            src_ref=st_ref,
            dst_ref=slots.at[k - 1],
            send_sem=send_sem.at[k - 1],
            recv_sem=recv_sem.at[k - 1],
            device_id=seq_device((me + k) % NSEQ, z),
            device_id_type=MESH,
        )
        copy.start()
        copies.append(copy)
    total = jnp.zeros((NS, SUB, LANE), F32)
    rate = rate_ref[...].reshape(NS, SUB, LANE)
    for k in range(REACH, 0, -1):
        copies[k - 1].wait_recv()
        block = slots[k - 1].astype(F32).reshape(NS + 2, SUB, LANE)
        steps = block[NS] + block[NS + 1]
        moved = jnp.exp2(rate * steps[None]) * total + block[:NS]
        total = jnp.where(me >= k, moved, 0.0)
    in_out[...] = total.reshape(NS * SUB, LANE)
    for copy in copies:
        copy.wait_send()


def enter(st, rate):
    dma = pltpu.SemaphoreType.DMA
    return pl.pallas_call(
        enter_kernel,
        out_shape=jax.ShapeDtypeStruct((NS * SUB, LANE), F32),
        in_specs=[whole()] * 2,
        out_specs=whole(),
        scratch_shapes=[VM((REACH, (NS + 2) * SUB, LANE), BF16), dma((REACH,)), dma((REACH,))],
        compiler_params=pltpu.CompilerParams(
            collective_id=1, has_side_effects=True, vmem_limit_bytes=VLIM
        ),
        name="enter",
    )(st, rate)


def output_kernel(
    in_ref, step_ref, drive_ref, rate_ref, proj_ref, inner_ref, z_ref, skip_ref, out, bcs, ys
):
    spread = spread_columns(proj_ref, RANK, 2 * NS)
    for n in range(2 * NS):
        bcs[pl.ds(n * TOK, TOK), :] = spread[:, n * LANE : (n + 1) * LANE]
    rates = [rate_ref[pl.ds(n * SUB, SUB), :] for n in range(NS)]

    def advance(t, carried):
        rows = pl.ds(pl.multiple_of(t * SUB, SUB), SUB)
        step = step_ref[rows, :]
        drive = drive_ref[rows, :]
        result = []
        total = None
        for n in range(NS):
            b = bcs[pl.ds(n * TOK + t, SUB, stride=0), :]
            weight = bcs[pl.ds((NS + n) * TOK + t, SUB, stride=0), :]
            state = jnp.exp2(step * rates[n]) * carried[n] + b * drive
            result.append(state)
            total = weight * state if total is None else total + weight * state
        ys[rows, :] = total
        return tuple(result)

    first = tuple(in_ref[pl.ds(n * SUB, SUB), :] for n in range(NS))
    lax.fori_loop(0, TOK, advance, first, unroll=4)
    for j in range(SUB):
        cols = pl.ds(j * LANE, LANE)
        scanned = ys[pl.ds(j, TOK, stride=SUB), :] + skip_ref[:, cols] * inner_ref[:, cols].astype(F32)
        out[:, cols] = (scanned * silu(z_ref[:, cols].astype(F32))).astype(BF16)


def scan_output(h_in, step, drive, rate, proj, inner, z, skip):
    return pl.pallas_call(
        output_kernel,
        out_shape=jax.ShapeDtypeStruct((TOK, CH), BF16),
        in_specs=[whole()] * 8,
        out_specs=whole(),
        scratch_shapes=[VM((2 * NS * TOK, LANE), F32), VM((TOK * SUB, LANE), F32)],
        compiler_params=pltpu.CompilerParams(vmem_limit_bytes=VLIM),
        name="scan_output",
    )(h_in, step, drive, rate, proj, inner, z, skip)


def attend_kernel(pos_ref, len_ref, q_ref, kv_ref, out):
    g = pl.program_id(0)
    heads = CH // HD
    rows = GROUP * RUN
    starts = doc_starts(len_ref)
    bases = [pos_ref[g * GROUP + i] for i in range(GROUP)]
    row = lax.broadcasted_iota(jnp.int32, (rows, BK), 0)
    col = lax.broadcasted_iota(jnp.int32, (rows, BK), 1)
    base = bases[0]
    for i in range(1, GROUP):
        base = jnp.where(row >= i * RUN, bases[i], base)
    pos = base + row % RUN
    start = start_of(pos, starts)
    first = start_of(bases[0], starts) // BK
    last = (bases[GROUP - 1] + RUN - 1) // BK
    q = jnp.concatenate([q_ref[:, h * HD : (h + 1) * HD] for h in range(heads)], axis=0)
    scale = HD**-0.5 * LOG2E

    def absorb(kb, carried):
        best, weight_sum, summed = carried
        key_rows = pl.ds(pl.multiple_of(kb * BK, BK), BK)
        keys = kv_ref[key_rows, pl.ds(0, HD)]
        values = kv_ref[key_rows, pl.ds(HD, HD)]
        scores = lax.dot_general(
            q, keys, (((1,), (1,)), ((), ())), preferred_element_type=F32
        ).reshape(heads, rows, BK)
        places = col + kb * BK
        visible = (places <= pos) & (places >= start)
        scores = jnp.where(visible[None], scores * scale, MASKED).reshape(heads * rows, BK)
        new_best = jnp.maximum(best, jnp.max(scores, axis=1, keepdims=True))
        weights = jnp.exp2(scores - new_best)
        rescale = jnp.exp2(best - new_best)
        weight_sum = weight_sum * rescale + jnp.sum(weights, axis=1, keepdims=True)
        product = jnp.dot(weights.astype(BF16), values, preferred_element_type=F32)
        return new_best, weight_sum, summed * rescale + product

    initial = (
        jnp.full((heads * rows, 1), MASKED, F32),
        jnp.zeros((heads * rows, 1), F32),
        jnp.zeros((heads * rows, HD), F32),
    )
    best, weight_sum, summed = lax.fori_loop(first, last + 1, absorb, initial)
    result = (summed / weight_sum).astype(BF16)
    for h in range(heads):
        out[:, h * HD : (h + 1) * HD] = result[h * rows : (h + 1) * rows]


def attend(positions, lengths, q, kv):
    rows = GROUP * RUN
    return pl.pallas_call(
        attend_kernel,
        out_shape=jax.ShapeDtypeStruct((TOK, CH), BF16),
        grid=(NSEQ // GROUP,),
        in_specs=[
            whole(pltpu.SMEM),
            whole(pltpu.SMEM),
            pl.BlockSpec((rows, CH), lambda g: (g, 0)),
            whole(),
        ],
        out_specs=pl.BlockSpec((rows, CH), lambda g: (g, 0)),
        compiler_params=pltpu.CompilerParams(vmem_limit_bytes=VLIM),
        name="attend",
    )(positions, lengths, q, kv)


def local(
    x_branch,
    z_branch,
    conv_weight,
    conv_bias,
    xproj_weight,
    dt_weight,
    dt_bias,
    decay_rate,
    skip_gain,
    query_rows,
    key_rows,
    value_rows,
    lengths,
    destination,
):
    me = lax.axis_index(SEQ)
    targets = destination.reshape(NSEQ, NSEQ, RUN)[:, :, 0] // TOK
    runs = jnp.arange(NSEQ, dtype=jnp.int32)
    own = lax.dynamic_slice_in_dim(targets, me, 1, 0)
    inverse = jnp.sum(jnp.where(own == runs[:, None], runs[None, :], 0), axis=1)
    positions = runs * TOK + RUN * jnp.sum(jnp.where(targets == me, runs[None, :], 0), axis=1)
    q, kv, proj, inner = gather_all(
        inverse,
        lengths,
        query_rows.reshape(NSEQ, RUN, CH),
        key_rows,
        value_rows,
        x_branch,
        conv_weight,
        conv_bias.reshape(1, CH),
        xproj_weight,
    )
    st, step, drive, rate = local_scan(
        lengths,
        me.reshape(1).astype(jnp.int32),
        proj,
        inner,
        dt_weight,
        dt_bias.reshape(1, CH),
        decay_rate,
    )
    h_in = enter(st, rate)
    mamba_out = scan_output(
        h_in, step, drive, rate, proj, inner, z_branch, skip_gain.reshape(1, CH)
    )
    regrouped = attend(positions, lengths, q, kv)
    return (mamba_out, regrouped)


def solution(mesh):
    torus = Mesh(mesh.devices.reshape(NX, NY, NC, mesh.shape["mp"]), (*SEQ, "mp"))
    in_specs = (
        P(SEQ, "mp"),
        P(SEQ, "mp"),
        P(None, "mp"),
        P("mp"),
        P("mp", None),
        P(None, "mp"),
        P("mp"),
        P(None, "mp"),
        P("mp"),
        P(SEQ, "mp"),
        P(SEQ, "mp"),
        P(SEQ, "mp"),
        P(),
        P(),
    )
    out_specs = (P(SEQ, "mp"), P(SEQ, "mp"))
    return jax.shard_map(local, mesh=torus, in_specs=in_specs, out_specs=out_specs, check_vma=False)
```

time: 531 us -> 119 us (0.22)
  the two profiles are of different devices: /device:TPU:32 before, /device:TPU:1 now
where the time goes in v1:
time: 119 us; the launch traced here: 117 us
  Pallas kernels  112 us (94%)
  local copies, waits for them, and re-layouts  3.21 us (3%)
  other arithmetic  1.28 us (1%)
    pallas_call x1, Pallas kernels, gather_all(): pl.pallas_call(gather_kernel, out_shape=(jax.ShapeDtypeStruct((TOK, CH),...  39.8 us
    pallas_call x1, Pallas kernels, attend(): pl.pallas_call(attend_kernel, out_shape=jax.ShapeDtypeStruct((TOK, CH), B...  36.7 us
    pallas_call x1, Pallas kernels, enter(): pl.pallas_call(enter_kernel, out_shape=jax.ShapeDtypeStruct((NS * SUB, LA...  18.8 us
    pallas_call x1, Pallas kernels, scan_output(): pl.pallas_call(output_kernel, out_shape=jax.ShapeDtypeStruct((TOK, CH), B...  8.69 us
    pallas_call x1, Pallas kernels, local_scan(): pl.pallas_call(local_scan_kernel, out_shape=(jax.ShapeDtypeStruct(((NS +...  7.85 us

profile of v1, /device:TPU:1, one launch (start us, length us, event | category | flops | bytes accessed | tf_op | source)
XLA Modules:
  0.0 117.0 jit_solution(16193770864015388090)
XLA Ops:
  0.6 0.0 copy-start
  0.6 1.1 reshape.23
  1.8 0.6 slice_reduce_fusion
  2.4 0.1 select_reduce_fusion
  2.5 0.5 multiply_add_fusion.pos_ref
  3.1 0.6 select_reduce_fusion.1.inv_ref
  3.7 0.0 copy-done
  3.7 1.4 %copy.18.xw_ref = bf16[1024,544]{1,0:T(8,128)(2,1)} copy(bf16[1024,544]{0,1:T(8,128)(2,1)S(1)} %copy-done) | data formatting | bytes 2228224 | tf_op args[4]
  5.1 39.8 %gather.1 = (bf16[256,1024]{1,0:T(8,128)(2,1)}, bf16[8192,256]{1,0:T(8,128)(2,1)}, bf16[256,544]{1,0:T(8,128)(2,1)}, bf16[256,1024]{1,0:T(8,128)(2,1)}) custom-call(s32[32]{0:T(128)} %select_reduce_fusion.1.inv_ref, s32[4]{0:T(128)} %len_ref.5, bf16[32,8,1024]{2,1,0:T(8,128)(2,1)} %bitcast.7, bf16[256,128]{1,0:T(8,128)(2,1)} %k_ref.1, ...), custom_call_target="tpu_custom_call" | custom-call | tf_op jit(solution)/shard_map/gather/pallas_call | solution.py:251
  44.9 36.7 %attend.1 = bf16[256,1024]{1,0:T(8,128)(2,1)} custom-call(s32[32]{0:T(128)} %multiply_add_fusion.pos_ref, s32[4]{0:T(128)} %len_ref.5, bf16[256,1024]{1,0:T(8,128)(2,1)} %get-tuple-element.16.q_ref, bf16[8192,256]{1,0:T(8,128)(2,1)} %get-tuple-element.17.kv_ref), custom_call_target="tpu_custom_call" | custom-call | tf_op jit(solution)/shard_map/attend/pallas_call | solution.py:498
  81.6 7.8 %local_scan.1 = (bf16[144,128]{1,0:T(8,128)(2,1)}, f32[2048,128]{1,0:T(8,128)}, f32[2048,128]{1,0:T(8,128)}, f32[128,128]{1,0:T(8,128)}) custom-call(s32[4]{0:T(128)} %len_ref.5, s32[1]{0:T(128)} %bitcast.me_ref, bf16[256,544]{1,0:T(8,128)(2,1)} %get-tuple-element.10.proj_ref, bf16[256,1024]{1,0:T(8,128)(2,1)} %get-tuple-element.11.inner_ref, ...), custom_call_target="tpu_custom_call" | custom-call | tf_op jit(solution)/shard_map/local_scan/pallas_call | solution.py:341
  89.5 18.8 %enter.1.in_ref = f32[128,128]{1,0:T(8,128)} custom-call(bf16[144,128]{1,0:T(8,128)(2,1)} %get-tuple-element.12.st_ref, f32[128,128]{1,0:T(8,128)} %get-tuple-element.13.rate_ref), custom_call_target="tpu_custom_call" | custom-call | tf_op jit(solution)/shard_map/enter/pallas_call | solution.py:393
  108.3 8.7 %scan_output.1 = bf16[256,1024]{1,0:T(8,128)(2,1)} custom-call(f32[128,128]{1,0:T(8,128)} %enter.1.in_ref, f32[2048,128]{1,0:T(8,128)} %get-tuple-element.14.step_ref, f32[2048,128]{1,0:T(8,128)} %get-tuple-element.15.drive_ref, f32[128,128]{1,0:T(8,128)} %get-tuple-element.13.rate_ref, bf16[256,544]{1,0:T(8,128)(2,1)} %get-tuple-element.10.proj_ref, ...), custom_call_target="tpu_custom_call" | custom-call | tf_op jit(solution)/shard_map/scan_output/pallas_call | solution.py:438
  (1 shorter events, 0.0 us)
Async XLA Ops:
  0.6 3.1 %copy-start = (bf16[1024,544]{0,1:T(8,128)(2,1)S(1)}, bf16[1024,544]{0,1:T(8,128)(2,1)}, u32[]{:S(2)}) copy-start(bf16[1024,544]{0,1:T(8,128)(2,1)} %param.18) | copy-start | bytes 3342340

commit v2 on v1

--- a/solution.py
+++ b/solution.py
@@ -28,9 +28,9 @@
 REACH = 16
 BIG_STEP = 1.0e7
 MASKED = -1.0e30
-GROUP = 4
+GROUP = 8
 RUN = TOK // NSEQ
-BK = 256
+BK = 512
 VLIM = 60 * 1024 * 1024
 
 
@@ -110,13 +110,12 @@
             barrier, inc=1, device_id=(x, y, c, (z + k) % NZ), device_id_type=MESH
         )
     load_k = pltpu.make_async_copy(k_ref, kvs.at[:, pl.ds(0, HD)], loc_sem.at[0])
-    load_v = pltpu.make_async_copy(v_ref, kvs.at[:, pl.ds(HD, HD)], loc_sem.at[1])
     load_k.start()
-    load_v.start()
+    for half in range(TOK // HD):
+        kvs[pl.ds(half * HD, HD), pl.ds(HD, HD)] = v_ref[pl.ds(half * HD, HD), :].T
     for j in range(NSEQ):
         qs[j] = q_ref[inv_ref[j]]
     load_k.wait()
-    load_v.wait()
     pl.semaphore_wait(barrier, NSEQ - 1 + NZ - 1)
 
     def remote(src, dst, send, recv, device):
@@ -256,10 +255,7 @@
             jax.ShapeDtypeStruct((TOK, PROJ), BF16),
             jax.ShapeDtypeStruct((TOK, CH), BF16),
         ),
-        in_specs=[whole(pltpu.SMEM)] * 2
-        + [whole()]
-        + [whole(pl.ANY)] * 2
-        + [whole()] * 4,
+        in_specs=[whole(pltpu.SMEM)] * 2 + [whole(), whole(pl.ANY)] + [whole()] * 5,
         out_specs=(whole(pl.ANY), whole(pl.ANY), whole(), whole()),
         scratch_shapes=[
             VM((TOK, 2 * HD), BF16),
@@ -446,49 +442,74 @@
     )(h_in, step, drive, rate, proj, inner, z, skip)
 
 
-def attend_kernel(pos_ref, len_ref, q_ref, kv_ref, out):
+def attend_kernel(pos_ref, len_ref, q_ref, kv_ref, out, scores_a, scores_b):
     g = pl.program_id(0)
     heads = CH // HD
     rows = GROUP * RUN
+    count = heads * rows
+    wide = 2 * BK
+    per = TOK * GROUP // wide
     starts = doc_starts(len_ref)
     bases = [pos_ref[g * GROUP + i] for i in range(GROUP)]
-    row = lax.broadcasted_iota(jnp.int32, (rows, BK), 0)
-    col = lax.broadcasted_iota(jnp.int32, (rows, BK), 1)
+    lane = lax.broadcasted_iota(jnp.int32, (1, LANE), 1) % rows
     base = bases[0]
     for i in range(1, GROUP):
-        base = jnp.where(row >= i * RUN, bases[i], base)
-    pos = base + row % RUN
+        base = jnp.where(lane >= i * RUN, bases[i], base)
+    pos = base + lane % RUN
     start = start_of(pos, starts)
-    first = start_of(bases[0], starts) // BK
-    last = (bases[GROUP - 1] + RUN - 1) // BK
+    top = g * per
+    first = jnp.minimum(start_of(bases[0], starts) // wide, top)
+    last_start = start_of(bases[GROUP - 1] + RUN - 1, starts)
+    plain = jnp.maximum(jnp.minimum((last_start + wide - 1) // wide, top), first)
     q = jnp.concatenate([q_ref[:, h * HD : (h + 1) * HD] for h in range(heads)], axis=0)
     scale = HD**-0.5 * LOG2E
-
-    def absorb(kb, carried):
-        best, weight_sum, summed = carried
-        key_rows = pl.ds(pl.multiple_of(kb * BK, BK), BK)
-        keys = kv_ref[key_rows, pl.ds(0, HD)]
-        values = kv_ref[key_rows, pl.ds(HD, HD)]
-        scores = lax.dot_general(
-            q, keys, (((1,), (1,)), ((), ())), preferred_element_type=F32
-        ).reshape(heads, rows, BK)
-        places = col + kb * BK
-        visible = (places <= pos) & (places >= start)
-        scores = jnp.where(visible[None], scores * scale, MASKED).reshape(heads * rows, BK)
-        new_best = jnp.maximum(best, jnp.max(scores, axis=1, keepdims=True))
-        weights = jnp.exp2(scores - new_best)
+    key_row = lax.broadcasted_iota(jnp.int32, (BK, LANE), 0)
+    ones = jnp.ones((16, BK), BF16)
+
+    def score(into, i):
+        keys = kv_ref[pl.ds(pl.multiple_of(i * BK, BK), BK), pl.ds(0, HD)]
+        into[...] = lax.dot_general(
+            keys, q, (((1,), (1,)), ((), ())), preferred_element_type=F32
+        )
+
+    def absorb(taken, i, carried, masked):
+        begin = pl.multiple_of(i * BK, BK)
+        best, summed = carried
+        scores = taken[...]
+        if masked:
+            visible = (key_row <= pos - begin) & (key_row >= start - begin)
+            scores = jnp.concatenate(
+                [
+                    jnp.where(visible, scores[:, j : j + LANE], MASKED)
+                    for j in range(0, count, LANE)
+                ],
+                axis=1,
+            )
+        new_best = jnp.maximum(best, jnp.max(scores, axis=0, keepdims=True) * scale)
+        weights = jnp.exp2(scores * scale - new_best).astype(BF16)
         rescale = jnp.exp2(best - new_best)
-        weight_sum = weight_sum * rescale + jnp.sum(weights, axis=1, keepdims=True)
-        product = jnp.dot(weights.astype(BF16), values, preferred_element_type=F32)
-        return new_best, weight_sum, summed * rescale + product
-
-    initial = (
-        jnp.full((heads * rows, 1), MASKED, F32),
-        jnp.zeros((heads * rows, 1), F32),
-        jnp.zeros((heads * rows, HD), F32),
-    )
-    best, weight_sum, summed = lax.fori_loop(first, last + 1, absorb, initial)
-    result = (summed / weight_sum).astype(BF16)
+        values = jnp.concatenate(
+            [kv_ref[pl.ds(begin + j, HD), pl.ds(HD, HD)] for j in range(0, BK, HD)], axis=1
+        )
+        values = jnp.concatenate([values, ones], axis=0)
+        product = jnp.dot(values, weights, preferred_element_type=F32)
+        return new_best, summed * rescale + product
+
+    def pair(i, carried, masked, more=True):
+        score(scores_b, 2 * i + 1)
+        carried = absorb(scores_a, 2 * i, carried, masked)
+        if more:
+            score(scores_a, 2 * i + 2)
+        return absorb(scores_b, 2 * i + 1, carried, masked)
+
+    carried = (jnp.full((1, count), MASKED * scale, F32), jnp.zeros((HD + 16, count), F32))
+    score(scores_a, 2 * first)
+    carried = lax.fori_loop(first, plain, lambda i, v: pair(i, v, True), carried)
+    carried = lax.fori_loop(plain, top, lambda i, v: pair(i, v, False), carried)
+    for i in range(per):
+        carried = pair(top + i, carried, True, i < per - 1)
+    summed = carried[1]
+    result = (summed[:HD] / summed[HD : HD + 1]).T.astype(BF16)
     for h in range(heads):
         out[:, h * HD : (h + 1) * HD] = result[h * rows : (h + 1) * rows]
 
@@ -506,6 +527,7 @@
             whole(),
         ],
         out_specs=pl.BlockSpec((rows, CH), lambda g: (g, 0)),
+        scratch_shapes=[VM((BK, CH // HD * rows), F32)] * 2,
         compiler_params=pltpu.CompilerParams(vmem_limit_bytes=VLIM),
         name="attend",
     )(positions, lengths, q, kv)

time: 119 us -> 98.3 us (0.83); the launches traced: 117 us -> 98.6 us
  Pallas kernels: 112 us -> 93.4 us
    pallas_call x1, Pallas kernels: 36.7 us -> 18.2 us  [attend(): pl.pallas_call(attend_kernel, out_shape=jax.ShapeDtypeStruct((TOK, CH), B...]
where the time goes in v2:
time: 98.3 us; the launch traced here: 98.6 us
  Pallas kernels  93.4 us (95%)
  local copies, waits for them, and re-layouts  3.21 us (3%)
  other arithmetic  1.28 us (1%)
    pallas_call x1, Pallas kernels, gather_all(): pl.pallas_call(gather_kernel, out_shape=(jax.ShapeDtypeStruct((TOK, CH),...  39.8 us
    pallas_call x1, Pallas kernels, enter(): pl.pallas_call(enter_kernel, out_shape=jax.ShapeDtypeStruct((NS * SUB, LA...  18.8 us
    pallas_call x1, Pallas kernels, attend(): pl.pallas_call(attend_kernel, out_shape=jax.ShapeDtypeStruct((TOK, CH), B...  18.2 us
    pallas_call x1, Pallas kernels, scan_output(): pl.pallas_call(output_kernel, out_shape=jax.ShapeDtypeStruct((TOK, CH), B...  8.69 us
    pallas_call x1, Pallas kernels, local_scan(): pl.pallas_call(local_scan_kernel, out_shape=(jax.ShapeDtypeStruct(((NS +...  7.85 us

profile of v2, /device:TPU:1, one launch (start us, length us, event | category | flops | bytes accessed | tf_op | source)
XLA Modules:
  0.0 98.6 jit_solution(12861769566189162186)
XLA Ops:
  0.6 0.0 copy-start
  0.6 1.1 %reshape.23 = s32[32,32,8]{2,1,0:T(8,128)S(1)} reshape(s32[8192]{0:T(1024)} %param.27) | data formatting | bytes 65536 | tf_op jit(solution)/shard_map/reshape | solution.py:553
  1.8 0.6 slice_reduce_fusion
  2.4 0.1 select_reduce_fusion
  2.5 0.5 multiply_add_fusion.pos_ref
  3.1 0.6 select_reduce_fusion.1.inv_ref
  3.7 0.0 copy-done
  3.7 1.4 %copy.18.xw_ref = bf16[1024,544]{1,0:T(8,128)(2,1)} copy(bf16[1024,544]{0,1:T(8,128)(2,1)S(1)} %copy-done) | data formatting | bytes 2228224 | tf_op args[4]
  5.1 39.8 %gather.1 = (bf16[256,1024]{1,0:T(8,128)(2,1)}, bf16[8192,256]{1,0:T(8,128)(2,1)}, bf16[256,544]{1,0:T(8,128)(2,1)}, bf16[256,1024]{1,0:T(8,128)(2,1)}) custom-call(s32[32]{0:T(128)} %select_reduce_fusion.1.inv_ref, s32[4]{0:T(128)} %len_ref.5, bf16[32,8,1024]{2,1,0:T(8,128)(2,1)} %bitcast.7, bf16[256,128]{1,0:T(8,128)(2,1)} %k_ref.1, ...), custom_call_target="tpu_custom_call" | custom-call | tf_op jit(solution)/shard_map/gather/pallas_call | solution.py:250
  45.0 18.2 %attend.1 = bf16[256,1024]{1,0:T(8,128)(2,1)} custom-call(s32[32]{0:T(128)} %multiply_add_fusion.pos_ref, s32[4]{0:T(128)} %len_ref.5, bf16[256,1024]{1,0:T(8,128)(2,1)} %get-tuple-element.16.q_ref, bf16[8192,256]{1,0:T(8,128)(2,1)} %get-tuple-element.17.kv_ref), custom_call_target="tpu_custom_call" | custom-call | tf_op jit(solution)/shard_map/attend/pallas_call | solution.py:519
  63.2 7.9 %local_scan.1 = (bf16[144,128]{1,0:T(8,128)(2,1)}, f32[2048,128]{1,0:T(8,128)}, f32[2048,128]{1,0:T(8,128)}, f32[128,128]{1,0:T(8,128)}) custom-call(s32[4]{0:T(128)} %len_ref.5, s32[1]{0:T(128)} %bitcast.me_ref, bf16[256,544]{1,0:T(8,128)(2,1)} %get-tuple-element.10.proj_ref, bf16[256,1024]{1,0:T(8,128)(2,1)} %get-tuple-element.11.inner_ref, ...), custom_call_target="tpu_custom_call" | custom-call | tf_op jit(solution)/shard_map/local_scan/pallas_call | solution.py:337
  71.0 18.8 %enter.1.in_ref = f32[128,128]{1,0:T(8,128)} custom-call(bf16[144,128]{1,0:T(8,128)(2,1)} %get-tuple-element.12.st_ref, f32[128,128]{1,0:T(8,128)} %get-tuple-element.13.rate_ref), custom_call_target="tpu_custom_call" | custom-call | tf_op jit(solution)/shard_map/enter/pallas_call | solution.py:389
  89.9 8.7 %scan_output.1 = bf16[256,1024]{1,0:T(8,128)(2,1)} custom-call(f32[128,128]{1,0:T(8,128)} %enter.1.in_ref, f32[2048,128]{1,0:T(8,128)} %get-tuple-element.14.step_ref, f32[2048,128]{1,0:T(8,128)} %get-tuple-element.15.drive_ref, f32[128,128]{1,0:T(8,128)} %get-tuple-element.13.rate_ref, bf16[256,544]{1,0:T(8,128)(2,1)} %get-tuple-element.10.proj_ref, ...), custom_call_target="tpu_custom_call" | custom-call | tf_op jit(solution)/shard_map/scan_output/pallas_call | solution.py:434
  (1 shorter events, 0.0 us)
Async XLA Ops:
  0.6 3.1 %copy-start = (bf16[1024,544]{0,1:T(8,128)(2,1)S(1)}, bf16[1024,544]{0,1:T(8,128)(2,1)}, u32[]{:S(2)}) copy-start(bf16[1024,544]{0,1:T(8,128)(2,1)} %param.18) | copy-start | bytes 3342340

commit v3 on v2

v3 whole, which is shorter than its diff:
```python
import math

import jax
import jax.numpy as jnp
from jax import lax
from jax.experimental import pallas as pl
from jax.experimental.pallas import tpu as pltpu
from jax.sharding import Mesh
from jax.sharding import PartitionSpec as P

SEQ = ("seq_0", "seq_1", "seq_2")
MESH = pl.DeviceIdType.MESH
VM = pltpu.VMEM
F32 = jnp.float32
BF16 = jnp.bfloat16
LOG2E = math.log2(math.e)
NX, NY, NC, NZ = 4, 4, 2, 8
NSEQ = NX * NY * NC
TOK = 256
CH = 1024
LANE = 128
SUB = CH // LANE
NS = 16
RANK = 512
PROJ = RANK + 2 * NS
HD = 128
TAPS = 4
BIG_STEP = 1.0e7
MASKED = -1.0e30
GROUP = 8
RUN = TOK // NSEQ
BK = 512
VLIM = 60 * 1024 * 1024


def whole(space=VM):
    return pl.BlockSpec(memory_space=space)


def place():
    return (
        lax.axis_index("seq_0"),
        lax.axis_index("seq_1"),
        lax.axis_index("seq_2"),
        lax.axis_index("mp"),
    )


def seq_device(j, z):
    return (j // (NY * NC), (j // NC) % NY, j % NC, z)


def doc_starts(len_ref):
    s1 = len_ref[0]
    s2 = s1 + len_ref[1]
    return s1, s2, s2 + len_ref[2]


def start_of(pos, starts):
    s1, s2, s3 = starts
    return jnp.where(pos >= s3, s3, jnp.where(pos >= s2, s2, jnp.where(pos >= s1, s1, 0)))


def silu(x):
    return x / (1.0 + jnp.exp(-x))


def mixer_kernel(
    dest_ref,
    len_ref,
    q_ref,
    k_ref,
    v_ref,
    x_ref,
    z_ref,
    cw_ref,
    cb_ref,
    xw_ref,
    dtw_ref,
    dtb_ref,
    rate_ref,
    skip_ref,
    q_out,
    kv_out,
    pos_out,
    out,
    kvs,
    qs,
    halo,
    ext,
    inner,
    part,
    rs_plus,
    rs_minus,
    go_plus,
    go_minus,
    proj,
    steps,
    drives,
    rates,
    spread,
    gains,
    ys,
    sums,
    st_own,
    st_pair,
    st_y,
    st_x,
    loc_sem,
    halo_sem,
    kv_send,
    kv_recv,
    q_send,
    q_recv,
    rs_send,
    rs_recv,
    ag_send,
    ag_recv,
    st_send,
    st_recv,
):
    x, y, c, z = place()
    me = (x * NY + y) * NC + c
    anchor = me * TOK
    barrier = pltpu.get_barrier_semaphore()
    for k in range(1, NSEQ):
        pl.semaphore_signal(
            barrier, inc=1, device_id=seq_device((me + k) % NSEQ, z), device_id_type=MESH
        )
    for k in range(1, NZ):
        pl.semaphore_signal(
            barrier, inc=1, device_id=(x, y, c, (z + k) % NZ), device_id_type=MESH
        )
    load_k = pltpu.make_async_copy(k_ref, kvs.at[:, pl.ds(0, HD)], loc_sem.at[0])
    load_k.start()
    for half in range(TOK // HD):
        kvs[pl.ds(half * HD, HD), pl.ds(HD, HD)] = v_ref[pl.ds(half * HD, HD), :].T

    def stage(j, carry):
        run = 0
        for r in range(NSEQ):
            run = jnp.where(dest_ref[anchor + r * RUN] // TOK == j, r, run)
        qs[j] = q_ref[run]
        return carry

    lax.fori_loop(0, NSEQ, stage, 0)

    starts = doc_starts(len_ref)
    token = anchor + lax.broadcasted_iota(jnp.int32, (TOK, LANE), 0)
    depth = token - start_of(token, starts)

    def convolve(count, cols, far):
        total = cb_ref[:, cols] + cw_ref[pl.ds(0, 1), cols] * ext[pl.ds(8, count), cols]
        for lag in range(1, TAPS):
            window = ext[pl.ds(8 - lag, count), cols]
            total = total + cw_ref[pl.ds(lag, 1), cols] * jnp.where(far >= lag, window, 0.0)
        inner[pl.ds(0, count), cols] = silu(total).astype(BF16)

    def conv_columns(i, carry):
        cols = pl.ds(pl.multiple_of(i * LANE, LANE), LANE)
        ext[pl.ds(0, 8), cols] = jnp.zeros((8, LANE), F32)
        ext[pl.ds(8, TOK), cols] = x_ref[:, cols].astype(F32)
        convolve(TOK, cols, depth)
        return carry

    lax.fori_loop(0, SUB, conv_columns, 0)
    load_k.wait()
    pl.semaphore_wait(barrier, NSEQ - 1 + NZ - 1)

    def remote(src, dst, send, recv, device):
        return pltpu.make_async_remote_copy(
            src_ref=src,
            dst_ref=dst,
            send_sem=send,
            recv_sem=recv,
            device_id=device,
            device_id_type=MESH,
        )

    def offset(a, b, core):
        return (x + a * (1 - core) + b * core) % NX, (y + a * core + b * (1 - core)) % NY

    def rows_of(a, b, core):
        px, py = offset(a, b, core)
        return pl.ds(pl.multiple_of(((px * NY + py) * NC + core) * TOK, TOK), TOK)

    partner = (x, y, 1 - c, z)
    after = (me + 1) % NSEQ
    halo_copy = remote(
        x_ref.at[pl.ds(TOK - 16, 16)], halo, halo_sem.at[0], halo_sem.at[1], seq_device(after, z)
    )
    halo_copy.start()
    mine = kv_out.at[rows_of(0, 0, c)]
    sends = []
    for a in range(1, NX):
        px, py = offset(a, 0, c)
        copy = remote(kvs, mine, kv_send.at[a], kv_recv.at[a], (px, py, c, z))
        copy.start()
        sends.append(copy)
    copy = remote(kvs, mine, kv_send.at[16], kv_recv.at[16], partner)
    copy.start()
    sends.append(copy)
    keep_kv = pltpu.make_async_copy(kvs, mine, loc_sem.at[0])
    keep_kv.start()
    q_rows = pl.ds(pl.multiple_of(me * RUN, RUN), RUN)
    for k in range(1, NSEQ):
        j = (me + k) % NSEQ
        copy = remote(qs.at[j], q_out.at[q_rows], q_send.at[k], q_recv.at[k], seq_device(j, z))
        copy.start()
        sends.append(copy)
    keep_q = pltpu.make_async_copy(qs.at[me], q_out.at[q_rows], loc_sem.at[1])
    keep_q.start()

    halo_copy.wait()
    ext[pl.ds(0, 8), :] = halo[pl.ds(8, 8), :].astype(F32)
    near = anchor + lax.broadcasted_iota(jnp.int32, (16, CH), 0)
    convolve(16, pl.ds(0, CH), near - start_of(near, starts))

    partial = lax.dot_general(
        inner[...], xw_ref[...], (((1,), (1,)), ((), ())), preferred_element_type=F32
    ).astype(BF16)
    slice_rows = TOK // NZ
    part[...] = partial.reshape(NZ, slice_rows, PROJ)
    up = (x, y, c, (z + 1) % NZ)
    down = (x, y, c, (z + NZ - 1) % NZ)

    def ring_plus(s):
        src = part.at[(z + 4) % NZ] if s == 1 else go_plus.at[s]
        return remote(src, rs_plus.at[s], rs_send.at[s], rs_recv.at[s], up)

    def ring_minus(s):
        src = part.at[(z + 5) % NZ] if s == 1 else go_minus.at[s]
        return remote(src, rs_minus.at[s], rs_send.at[4 + s], rs_recv.at[4 + s], down)

    plus, minus = ring_plus(1), ring_minus(1)
    plus.start()
    minus.start()
    sends += [plus, minus]

    def wait_kv(slot_rows, index):
        remote(kvs, kv_out.at[slot_rows], kv_send.at[0], kv_recv.at[index], partner).wait_recv()

    for s in range(1, 4):
        plus.wait_recv()
        go_plus[s + 1] = (rs_plus[s].astype(F32) + part[(z + 4 - s) % NZ].astype(F32)).astype(BF16)
        plus = ring_plus(s + 1)
        plus.start()
        sends.append(plus)
        minus.wait_recv()
        if s < 3:
            go_minus[s + 1] = (
                rs_minus[s].astype(F32) + part[(z + 5 + s) % NZ].astype(F32)
            ).astype(BF16)
            minus = ring_minus(s + 1)
            minus.start()
            sends.append(minus)
        if s == 1:
            for a in range(NX):
                if a > 0:
                    wait_kv(rows_of(-a, 0, c), a)
                block = kv_out.at[rows_of(-a, 0, c)] if a > 0 else kvs
                target = kv_out.at[rows_of(-a, 0, c)]
                for b in range(1, NY):
                    px, py = offset(0, b, c)
                    index = b * NX + a
                    copy = remote(
                        block, target, kv_send.at[index], kv_recv.at[index], (px, py, c, z)
                    )
                    copy.start()
                    sends.append(copy)
                if a > 0:
                    copy = remote(
                        block, target, kv_send.at[16 + a], kv_recv.at[16 + a], partner
                    )
                    copy.start()
                    sends.append(copy)
    plus.wait_recv()
    total = part[z].astype(F32) + rs_plus[4].astype(F32) + rs_minus[3].astype(F32)

    def proj_rows(chunk):
        return pl.ds(pl.multiple_of((chunk % NZ) * slice_rows, slice_rows), slice_rows)

    proj[proj_rows(z), :] = total.astype(BF16)

    def pass_plus(s):
        rows = proj.at[proj_rows(z + NZ + 1 - s)]
        return remote(rows, rows, ag_send.at[s], ag_recv.at[s], up)

    def pass_minus(s):
        rows = proj.at[proj_rows(z + s - 1)]
        return remote(rows, rows, ag_send.at[4 + s], ag_recv.at[4 + s], down)

    def got_plus(s):
        rows = proj.at[proj_rows(z + NZ - s)]
        remote(rows, rows, ag_send.at[s], ag_recv.at[s], up).wait_recv()

    def got_minus(s):
        rows = proj.at[proj_rows(z + s)]
        remote(rows, rows, ag_send.at[4 + s], ag_recv.at[4 + s], down).wait_recv()

    for s in range(1, 5):
        if s > 1:
            got_plus(s - 1)
        copy = pass_plus(s)
        copy.start()
        sends.append(copy)
        if s < 4:
            if s > 1:
                got_minus(s - 1)
            copy = pass_minus(s)
            copy.start()
            sends.append(copy)
    for j in range(SUB):
        cols = pl.ds(j * LANE, LANE)
        rates[pl.ds(j, NS, stride=SUB), :] = rate_ref[:, cols] * (-LOG2E)
    got_minus(3)
    got_plus(4)

    begins = depth == 0
    for j in range(SUB):
        cols = pl.ds(j * LANE, LANE)
        raw = jnp.dot(proj[:, pl.ds(0, RANK)], dtw_ref[:, cols], preferred_element_type=F32)
        step = jax.nn.softplus(raw + dtb_ref[:, cols])
        drives[pl.ds(j, TOK, stride=SUB), :] = step * inner[:, cols].astype(F32)
        step = jnp.where(begins, BIG_STEP, step)
        sums[pl.ds(j, 1), :] = jnp.sum(step, axis=0, keepdims=True)
        steps[pl.ds(j, TOK, stride=SUB), :] = step
    row = lax.broadcasted_iota(jnp.int32, (2 * NS, 2 * NS * LANE), 0)
    col = lax.broadcasted_iota(jnp.int32, (2 * NS, 2 * NS * LANE), 1)
    pick = jnp.where(col // LANE == row, 1.0, 0.0).astype(BF16)
    wide = jnp.dot(proj[:, pl.ds(RANK, 2 * NS)], pick, preferred_element_type=F32)
    for n in range(2 * NS):
        spread[pl.ds(n * TOK, TOK), :] = wide[:, n * LANE : (n + 1) * LANE]
    rate = [rates[pl.ds(n * SUB, SUB), :] for n in range(NS)]

    def advance(t, carried):
        rows = pl.ds(pl.multiple_of(t * SUB, SUB), SUB)
        step = steps[rows, :]
        drive = drives[rows, :]
        result = []
        for n in range(NS):
            b = spread[pl.ds(n * TOK + t, SUB, stride=0), :]
            result.append(jnp.exp2(step * rate[n]) * carried[n] + b * drive)
        return tuple(result)

    zero = jnp.zeros((SUB, LANE), F32)
    state = lax.fori_loop(0, TOK, advance, (zero,) * NS, unroll=4)

    def pack(into, states, total):
        for n in range(0, NS, 2):
            pair = jnp.concatenate([states[n], states[n + 1]], axis=0)
            into[pl.ds(n * SUB, 2 * SUB), :] = pair.astype(BF16)
        high = total.astype(BF16).astype(F32)
        pair = jnp.concatenate([high, total - high], axis=0)
        into[pl.ds(NS * SUB, 2 * SUB), :] = pair.astype(BF16)

    def unpack(taken):
        block = taken[...].astype(F32).reshape(NS + 2, SUB, LANE)
        return [block[n] for n in range(NS)], block[NS] + block[NS + 1]

    def follow(states, block, total, passed=None):
        result = []
        for n in range(NS):
            moved = jnp.exp2(rate[n] * total) * states[n] + block[n]
            result.append(moved if passed is None else jnp.where(passed, moved, states[n]))
        return result

    pack(st_own, state, sums[...])
    pair_copy = remote(st_own, st_pair, st_send.at[0], st_recv.at[0], partner)
    pair_copy.start()
    sends.append(pair_copy)

    def local_token(t, carried):
        so_far, states = carried
        rows = pl.ds(pl.multiple_of(t * SUB, SUB), SUB)
        step = steps[rows, :]
        drive = drives[rows, :]
        so_far = so_far + step
        result = []
        total = None
        for n in range(NS):
            r = rates[pl.ds(n * SUB, SUB), :]
            b = spread[pl.ds(n * TOK + t, SUB, stride=0), :]
            weight = spread[pl.ds((NS + n) * TOK + t, SUB, stride=0), :]
            new = jnp.exp2(step * r) * states[n] + b * drive
            result.append(new)
            total = weight * new if total is None else total + weight * new
            gains[t, pl.ds(n * SUB, SUB), :] = weight * jnp.exp2(so_far * r)
        ys[rows, :] = total
        return so_far, tuple(result)

    carried = (zero, (zero,) * NS)
    cuts = (0, 40, 144, TOK)
    carried = lax.fori_loop(cuts[0], cuts[1], local_token, carried, unroll=2)

    pair_copy.wait_recv()
    own_state, own_total = unpack(st_own)
    other_state, other_total = unpack(st_pair)
    first_core = c == 0
    early = [jnp.where(first_core, p, q) for p, q in zip(own_state, other_state)]
    late = [jnp.where(first_core, q, p) for p, q in zip(own_state, other_state)]
    late_total = jnp.where(first_core, other_total, own_total)
    chip_state = follow(early, late, late_total)
    pack(st_y.at[0], chip_state, own_total + other_total)
    level = []
    for k in range(1, NY):
        copy = remote(
            st_y.at[0], st_y.at[k], st_send.at[k], st_recv.at[k], (x, (y + k) % NY, c, z)
        )
        copy.start()
        level.append(copy)
    sends += level
    carried = lax.fori_loop(cuts[1], cuts[2], local_token, carried, unroll=2)

    for copy in level:
        copy.wait_recv()
    column, column_total = unpack(st_y.at[(y + NY) % NY])
    for j in range(1, NY):
        block, total = unpack(st_y.at[(y + NY - j) % NY])
        column = follow(column, block, total)
        column_total = column_total + total
    pack(st_x.at[0], column, column_total)
    level = []
    for k in range(1, NX):
        copy = remote(
            st_x.at[0], st_x.at[k], st_send.at[4 + k], st_recv.at[4 + k], ((x + k) % NX, y, c, z)
        )
        copy.start()
        level.append(copy)
    sends += level
    carried = lax.fori_loop(cuts[2], cuts[3], local_token, carried, unroll=2)

    for b in range(1, NY):
        for a in range(NX):
            index = b * NX + a
            wait_kv(rows_of(-a, -b, c), index)
            block = kv_out.at[rows_of(-a, -b, c)]
            copy = remote(block, block, kv_send.at[16 + index], kv_recv.at[16 + index], partner)
            copy.start()
            sends.append(copy)

    for copy in level:
        copy.wait_recv()
    entering = [zero] * NS
    for j in range(NX - 1):
        block, total = unpack(st_x.at[(x + NX - j) % NX])
        entering = follow(entering, block, total, x > j)
    for j in range(NY - 1):
        block, total = unpack(st_y.at[(y + NY - j) % NY])
        entering = follow(entering, block, total, y > j)
    entering = follow(entering, early, jnp.where(first_core, own_total, other_total), c > 0)

    def correct(t, carry):
        rows = pl.ds(pl.multiple_of(t * SUB, SUB), SUB)
        total = ys[rows, :]
        for n in range(NS):
            total = total + gains[t, pl.ds(n * SUB, SUB), :] * entering[n]
        ys[rows, :] = total
        return carry

    lax.fori_loop(0, TOK, correct, 0, unroll=4)
    for j in range(SUB):
        cols = pl.ds(j * LANE, LANE)
        scanned = ys[pl.ds(j, TOK, stride=SUB), :]
        scanned = scanned + skip_ref[:, cols] * inner[:, cols].astype(F32)
        out[:, cols] = (scanned * silu(z_ref[:, cols].astype(F32))).astype(BF16)

    def locate(i, carry):
        run = 0
        for r in range(NSEQ):
            run = jnp.where(dest_ref[i * TOK + r * RUN] // TOK == me, r, run)
        pos_out[i] = i * TOK + run * RUN
        return carry

    lax.fori_loop(0, NSEQ, locate, 0)
    for k in range(1, NSEQ):
        rows = pl.ds(pl.multiple_of(((me + NSEQ - k) % NSEQ) * RUN, RUN), RUN)
        remote(qs.at[0], q_out.at[rows], q_send.at[k], q_recv.at[k], partner).wait_recv()
    for b in range(NY):
        for a in range(NX):
            wait_kv(rows_of(-a, -b, 1 - c), 16 + b * NX + a)
    for copy in sends:
        copy.wait_send()
    keep_kv.wait()
    keep_q.wait()


def mix(dest, lengths, q, k, v, x, z, cw, cb, xw, dtw, dtb, rate, skip):
    dma = pltpu.SemaphoreType.DMA
    states = ((NS + 2) * SUB, LANE)
    chunk = (TOK // NZ, PROJ)
    return pl.pallas_call(
        mixer_kernel,
        out_shape=(
            jax.ShapeDtypeStruct((TOK, CH), BF16),
            jax.ShapeDtypeStruct((NSEQ * TOK, 2 * HD), BF16),
            jax.ShapeDtypeStruct((NSEQ,), jnp.int32),
            jax.ShapeDtypeStruct((TOK, CH), BF16),
        ),
        in_specs=[whole(pltpu.SMEM)] * 2 + [whole(), whole(pl.ANY)] + [whole()] * 10,
        out_specs=(whole(pl.ANY), whole(pl.ANY), whole(pltpu.SMEM), whole()),
        scratch_shapes=[
            VM((TOK, 2 * HD), BF16),
            VM((NSEQ, RUN, CH), BF16),
            VM((16, CH), BF16),
            VM((TOK + 8, CH), F32),
            VM((TOK, CH), BF16),
            VM((NZ, *chunk), BF16),
            VM((5, *chunk), BF16),
            VM((4, *chunk), BF16),
            VM((5, *chunk), BF16),
            VM((4, *chunk), BF16),
            VM((TOK, PROJ), BF16),
            VM((TOK * SUB, LANE), F32),
            VM((TOK * SUB, LANE), F32),
            VM((NS * SUB, LANE), F32),
            VM((2 * NS * TOK, LANE), F32),
            VM((TOK, NS * SUB, LANE), F32),
            VM((TOK * SUB, LANE), F32),
            VM((SUB, LANE), F32),
            VM(states, BF16),
            VM(states, BF16),
            VM((NY, *states), BF16),
            VM((NX, *states), BF16),
            dma((2,)),
            dma((2,)),
            dma((32,)),
            dma((32,)),
            dma((NSEQ,)),
            dma((NSEQ,)),
            dma((NZ,)),
            dma((NZ,)),
            dma((NZ,)),
            dma((NZ,)),
            dma((NZ,)),
            dma((NZ,)),
        ],
        compiler_params=pltpu.CompilerParams(
            collective_id=0, has_side_effects=True, vmem_limit_bytes=VLIM
        ),
        name="mixer",
    )(dest, lengths, q, k, v, x, z, cw, cb, xw, dtw, dtb, rate, skip)


def attend_kernel(pos_ref, len_ref, q_ref, kv_ref, out, scores_a, scores_b):
    g = pl.program_id(0)
    heads = CH // HD
    rows = GROUP * RUN
    count = heads * rows
    wide = 2 * BK
    per = TOK * GROUP // wide
    starts = doc_starts(len_ref)
    bases = [pos_ref[g * GROUP + i] for i in range(GROUP)]
    lane = lax.broadcasted_iota(jnp.int32, (1, LANE), 1) % rows
    base = bases[0]
    for i in range(1, GROUP):
        base = jnp.where(lane >= i * RUN, bases[i], base)
    pos = base + lane % RUN
    start = start_of(pos, starts)
    top = g * per
    first = jnp.minimum(start_of(bases[0], starts) // wide, top)
    last_start = start_of(bases[GROUP - 1] + RUN - 1, starts)
    plain = jnp.maximum(jnp.minimum((last_start + wide - 1) // wide, top), first)
    q = jnp.concatenate([q_ref[:, h * HD : (h + 1) * HD] for h in range(heads)], axis=0)
    scale = HD**-0.5 * LOG2E
    key_row = lax.broadcasted_iota(jnp.int32, (BK, LANE), 0)
    ones = jnp.ones((16, BK), BF16)

    def score(into, i):
        keys = kv_ref[pl.ds(pl.multiple_of(i * BK, BK), BK), pl.ds(0, HD)]
        into[...] = lax.dot_general(
            keys, q, (((1,), (1,)), ((), ())), preferred_element_type=F32
        )

    def absorb(taken, i, carried, masked):
        begin = pl.multiple_of(i * BK, BK)
        best, summed = carried
        scores = taken[...]
        if masked:
            visible = (key_row <= pos - begin) & (key_row >= start - begin)
            scores = jnp.concatenate(
                [
                    jnp.where(visible, scores[:, j : j + LANE], MASKED)
                    for j in range(0, count, LANE)
                ],
                axis=1,
            )
        new_best = jnp.maximum(best, jnp.max(scores, axis=0, keepdims=True) * scale)
        weights = jnp.exp2(scores * scale - new_best).astype(BF16)
        rescale = jnp.exp2(best - new_best)
        values = jnp.concatenate(
            [kv_ref[pl.ds(begin + j, HD), pl.ds(HD, HD)] for j in range(0, BK, HD)], axis=1
        )
        values = jnp.concatenate([values, ones], axis=0)
        product = jnp.dot(values, weights, preferred_element_type=F32)
        return new_best, summed * rescale + product

    def pair(i, carried, masked, more=True):
        score(scores_b, 2 * i + 1)
        carried = absorb(scores_a, 2 * i, carried, masked)
        if more:
            score(scores_a, 2 * i + 2)
        return absorb(scores_b, 2 * i + 1, carried, masked)

    carried = (jnp.full((1, count), MASKED * scale, F32), jnp.zeros((HD + 16, count), F32))
    score(scores_a, 2 * first)
    carried = lax.fori_loop(first, plain, lambda i, v: pair(i, v, True), carried)
    carried = lax.fori_loop(plain, top, lambda i, v: pair(i, v, False), carried)
    for i in range(per):
        carried = pair(top + i, carried, True, i < per - 1)
    summed = carried[1]
    result = (summed[:HD] / summed[HD : HD + 1]).T.astype(BF16)
    for h in range(heads):
        out[:, h * HD : (h + 1) * HD] = result[h * rows : (h + 1) * rows]


def attend(positions, lengths, q, kv):
    rows = GROUP * RUN
    return pl.pallas_call(
        attend_kernel,
        out_shape=jax.ShapeDtypeStruct((TOK, CH), BF16),
        grid=(NSEQ // GROUP,),
        in_specs=[
            whole(pltpu.SMEM),
            whole(pltpu.SMEM),
            pl.BlockSpec((rows, CH), lambda g: (g, 0)),
            whole(),
        ],
        out_specs=pl.BlockSpec((rows, CH), lambda g: (g, 0)),
        scratch_shapes=[VM((BK, CH // HD * rows), F32)] * 2,
        compiler_params=pltpu.CompilerParams(vmem_limit_bytes=VLIM),
        name="attend",
    )(positions, lengths, q, kv)


def local(
    x_branch,
    z_branch,
    conv_weight,
    conv_bias,
    xproj_weight,
    dt_weight,
    dt_bias,
    decay_rate,
    skip_gain,
    query_rows,
    key_rows,
    value_rows,
    lengths,
    destination,
):
    q, kv, positions, mamba_out = mix(
        destination,
        lengths,
        query_rows.reshape(NSEQ, RUN, CH),
        key_rows,
        value_rows,
        x_branch,
        z_branch,
        conv_weight,
        conv_bias.reshape(1, CH),
        xproj_weight.T,
        dt_weight,
        dt_bias.reshape(1, CH),
        decay_rate,
        skip_gain.reshape(1, CH),
    )
    regrouped = attend(positions, lengths, q, kv)
    return (mamba_out, regrouped)


def solution(mesh):
    torus = Mesh(mesh.devices.reshape(NX, NY, NC, mesh.shape["mp"]), (*SEQ, "mp"))
    in_specs = (
        P(SEQ, "mp"),
        P(SEQ, "mp"),
        P(None, "mp"),
        P("mp"),
        P("mp", None),
        P(None, "mp"),
        P("mp"),
        P(None, "mp"),
        P("mp"),
        P(SEQ, "mp"),
        P(SEQ, "mp"),
        P(SEQ, "mp"),
        P(),
        P(),
    )
    out_specs = (P(SEQ, "mp"), P(SEQ, "mp"))
    return jax.shard_map(local, mesh=torus, in_specs=in_specs, out_specs=out_specs, check_vma=False)
```

time: 98.3 us -> 87.4 us (0.89)
  Pallas kernels: 93.4 us -> 86.7 us
  local copies, waits for them, and re-layouts: 3.21 us -> 0.8 us
  other arithmetic: 1.28 us -> 0 us
    pallas_call x4 -> x1, Pallas kernels: 75.2 us -> 69.3 us  [mix(): pl.pallas_call(mixer_kernel, out_shape=(jax.ShapeDtypeStruct((TOK, CH), B...]
    reshape x1 -> x0, local copies, waits for them, and re-layouts: 1.14 us -> none  [local(): targets = destination.reshape(NSEQ, NSEQ, RUN)[:, :, 0] // TOK]
where the time goes in v3:
time: 87.4 us; the launch traced here: 88.1 us
  Pallas kernels  86.7 us (99%)
    pallas_call x1, Pallas kernels, mix(): pl.pallas_call(mixer_kernel, out_shape=(jax.ShapeDtypeStruct((TOK, CH), B...  69.3 us
    pallas_call x1, Pallas kernels, attend(): pl.pallas_call(attend_kernel, out_shape=jax.ShapeDtypeStruct((TOK, CH), B...  17.3 us

profile of v3, /device:TPU:1, one launch (start us, length us, event | category | flops | bytes accessed | tf_op | source)
XLA Modules:
  0.0 88.1 jit_solution(16712778899167123561)
XLA Ops:
  0.6 69.3 %mixer.1 = (bf16[256,1024]{1,0:T(8,128)(2,1)}, bf16[8192,256]{1,0:T(8,128)(2,1)}, s32[32]{0:T(128)}, bf16[256,1024]{1,0:T(8,128)(2,1)}) custom-call(s32[8192]{0:T(1024)} %dest_ref.1, s32[4]{0:T(128)} %len_ref.3, bf16[32,8,1024]{2,1,0:T(8,128)(2,1)} %bitcast.6, bf16[256,128]{1,0:T(8,128)(2,1)} %k_ref.1, bf16[256,128]{1,0:T(8,128)(2,1)} %v_ref.1, ...), custom_call_target="tpu_custom_call" | custom-call | tf_op jit(solution)/shard_map/mixer/pallas_call | solution.py:492
  70.0 0.0 copy-start
  70.0 17.3 %attend.1 = bf16[256,1024]{1,0:T(8,128)(2,1)} custom-call(s32[32]{0:T(128)} %get-tuple-element.7.pos_ref, s32[4]{0:T(128)} %len_ref.3, bf16[256,1024]{1,0:T(8,128)(2,1)} %get-tuple-element.8.q_ref, bf16[8192,256]{1,0:T(8,128)(2,1)} %get-tuple-element.9.kv_ref), custom_call_target="tpu_custom_call" | custom-call | tf_op jit(solution)/shard_map/attend/pallas_call | solution.py:619
  87.3 0.0 copy-done
  87.3 0.8 copy.17
Async XLA Ops:
  70.0 17.3 %copy-start = (bf16[256,1024]{1,0:T(8,128)(2,1)S(1)}, bf16[256,1024]{1,0:T(8,128)(2,1)}, u32[]{:S(2)}) copy-start(bf16[256,1024]{1,0:T(8,128)(2,1)} %get-tuple-element.12) | copy-start | bytes 1572868
